TPU v7x, 256 devices: a whole 4x4x8 slice. The times are simulated.
256 devices in a mesh: load: 16 (over x, z_hi), space: 16 (over y, z_lo, core).
Axes of the slice: x: 4, y: 4, z: 8 (z_hi: 4, z_lo: 2; z = z_hi * 2 + z_lo), core: 2. Of those that a mesh axis runs over, the one named last changes fastest.
Arguments:
- density: float32 [32, 32, 256], P('space', 'load'), may hold values from 0.3 to 1
- fixed_mask: int32 [32, 32, 256], P('space'), may hold values 0 or 1
- patch_index: int32 [32, 32, 256], P('space'), may hold values from 0 to 15
- patch_force: float32 [16, 3, 16], P('load'), may hold values from -6 to 6
Outputs:
- displacement: float32 [16, 3, 32, 32, 256], P('load', None, 'space')
- sensitivity: float32 [32, 32, 256], P('space', 'load')
Inputs may be any that keep to these rules, and one draw needn't show every extreme that they name: `fixed_mask`: 1 marks a node held fixed.
All inputs are finite; a program needn't handle non-finite values. No bound on the sum of `fixed_mask` on one device may be relied on, other than what follows from the above.
Results may differ from a plain program's by a relative error of at most 0.00027.
Values sent between devices are 32-bit elements; how exact they have to be, the bound alone decides.
No kernel may reach another device: no remote copies, remote signals or barrier semaphores. Data moves between devices by JAX's collectives and lax.ppermute only.
A program may use at most 64 MiB of HBM per device.

v0:
```python
import jax
import jax.numpy as jnp
from jax import lax
from jax.experimental import pallas as pl
from jax.experimental.pallas import tpu as pltpu
from jax.sharding import PartitionSpec as P

NX, NY, NZ = 32, 32, 256
PATCHES = 16
LOADS = 16
OUTSIDE = 16.0
void_stiffness = 0.001
poisson_ratio = 0.3
LAME = poisson_ratio / ((1.0 + poisson_ratio) * (1.0 - 2.0 * poisson_ratio))
SHEAR = 0.5 / (1.0 + poisson_ratio)
DIAGONAL = (LAME + 4.0 * SHEAR) / 9.0
MODE_SCALE = 1.0 / 16.0


def next_y(v, last):
    return jnp.where(last, 0.0, pltpu.roll(v, v.shape[0] - 1, 0))


def prev_y(v, first):
    return jnp.where(first, 0.0, pltpu.roll(v, 1, 0))


def next_z(v, last):
    return jnp.where(last, 0.0, pltpu.roll(v, v.shape[1] - 1, 1))


def prev_z(v, first):
    return jnp.where(first, 0.0, pltpu.roll(v, 1, 1))


def plane_edges():
    row = lax.broadcasted_iota(jnp.int32, (NY, NZ), 0)
    col = lax.broadcasted_iota(jnp.int32, (NY, NZ), 1)
    return row == 0, row == NY - 1, col == 0, col == NZ - 1


def plane_modes(v, y_last, z_last):
    ahead = next_z(v, z_last)
    out = []
    pair = (v + ahead, ahead - v)
    for part in pair:
        above = next_y(part, y_last)
        out.append((part + above, above - part))
    return [out[r][q] for q in range(2) for r in range(2)]


def element_modes(low, high):
    modes = {}
    for comp in range(3):
        for q in range(2):
            for r in range(2):
                a, b = low[4 * comp + 2 * q + r], high[4 * comp + 2 * q + r]
                if q + r > 0:
                    modes[comp, 0, q, r] = a + b
                modes[comp, 1, q, r] = b - a
    return modes


UNIT = ((1, 0, 0), (0, 1, 0), (0, 0, 1))
PAIRS = ((0, 1), (0, 2), (1, 2))


def both(i, j):
    return tuple(UNIT[i][k] + UNIT[j][k] for k in range(3))


BLOCKS = tuple(((i, both(i, j)), (k, both(k, j))) for j in range(3) for i, k in PAIRS if j not in (i, k))
TRIPLE = tuple((i, both(*[k for k in range(3) if k != i])) for i in range(3))


def mode_forces(h):
    out = {}
    trace = (h[(0,) + UNIT[0]] + h[(1,) + UNIT[1]] + h[(2,) + UNIT[2]]) * LAME
    for i in range(3):
        out[(i,) + UNIT[i]] = trace + (2.0 * SHEAR) * h[(i,) + UNIT[i]]
    for i, k in PAIRS:
        shear = SHEAR * (h[(i,) + UNIT[k]] + h[(k,) + UNIT[i]])
        out[(i,) + UNIT[k]] = shear
        out[(k,) + UNIT[i]] = shear
    for (i, a), (k, b) in BLOCKS:
        both_ = (LAME / 3.0) * (h[(i,) + a] + h[(k,) + b])
        out[(i,) + a] = both_ + SHEAR * h[(i,) + a]
        out[(k,) + b] = both_ + SHEAR * h[(k,) + b]
    total = h[(0,) + TRIPLE[0][1]] + h[(1,) + TRIPLE[1][1]] + h[(2,) + TRIPLE[2][1]]
    for i, a in TRIPLE:
        out[(i,) + a] = (SHEAR / 3.0) * (total + h[(i,) + a])
    for i in range(3):
        out[i, 1, 1, 1] = DIAGONAL * h[i, 1, 1, 1]
    return out


def mode_energy(h):
    trace = h[(0,) + UNIT[0]] + h[(1,) + UNIT[1]] + h[(2,) + UNIT[2]]
    summed = LAME * (trace * trace)
    normal = None
    for i in range(3):
        term = h[(i,) + UNIT[i]] * h[(i,) + UNIT[i]]
        normal = term if normal is None else normal + term
    summed = summed + (2.0 * SHEAR) * normal
    shear = None
    for i, k in PAIRS:
        pair = h[(i,) + UNIT[k]] + h[(k,) + UNIT[i]]
        term = pair * pair
        shear = term if shear is None else shear + term
    for (i, a), (k, b) in BLOCKS:
        shear = shear + (h[(i,) + a] * h[(i,) + a] + h[(k,) + b] * h[(k,) + b])
    blocks = None
    for (i, a), (k, b) in BLOCKS:
        pair = h[(i,) + a] + h[(k,) + b]
        term = pair * pair
        blocks = term if blocks is None else blocks + term
    summed = summed + SHEAR * shear + (LAME / 3.0) * blocks
    total = h[(0,) + TRIPLE[0][1]] + h[(1,) + TRIPLE[1][1]] + h[(2,) + TRIPLE[2][1]]
    triple = total * total
    corner = None
    for i, a in TRIPLE:
        triple = triple + h[(i,) + a] * h[(i,) + a]
        term = h[i, 1, 1, 1] * h[i, 1, 1, 1]
        corner = term if corner is None else corner + term
    return summed + (SHEAR / 3.0) * triple + DIAGONAL * corner


def krylov_kernel(slab, table, gathered, basis, moments, rows, weight, inverse, mass, w0, w1, w2, planes, layers):
    first = 2 * slab[0] - 3
    y_first, y_last, z_first, z_last = plane_edges()

    for load in range(LOADS):
        rows[:, 2 * load : 2 * load + 2, :] = gathered[load]

    def set_weight(i, _):
        layer = first - 1 + i
        inside = jnp.where((layer >= 0) & (layer < NX), 1.0, 0.0)
        rho = rows[i]
        weight[i] = (MODE_SCALE * inside) * (void_stiffness + (1.0 - void_stiffness) * (rho * rho * rho))
        return 0

    lax.fori_loop(0, 9, set_weight, 0)

    def set_plane(i, _):
        both_layers = weight[i] + weight[i + 1]
        across = both_layers + prev_y(both_layers, y_first)
        diag = (DIAGONAL / MODE_SCALE) * (across + prev_z(across, z_first))
        code = rows[9 + i]
        inv = jnp.where(code < OUTSIDE - 0.5, 1.0 / diag, 0.0)
        inverse[i] = inv
        mass[i] = diag
        scaled = inv * (1.0 + 2.0 * (first + i).astype(jnp.float32) / (NX - 1))
        for comp in range(3):
            force = jnp.zeros((NY, NZ), jnp.float32)
            for patch in range(PATCHES):
                force = jnp.where(code == float(patch), table[comp, patch], force)
            w0[comp, i] = scaled * force
        return 0

    lax.fori_loop(0, 8, set_plane, 0)

    def shifted_operator(source, target, count, lead):
        def to_modes(i, _):
            for comp in range(3):
                for k, part in enumerate(plane_modes(source[comp, i], y_last, z_last)):
                    planes[i, 4 * comp + k] = part
            return 0

        lax.fori_loop(0, count + 2, to_modes, 0)

        def column(tile, _):
            y = pl.ds(pl.multiple_of(tile * 8, 8), 8)
            for half in range(NZ // 128):
                z = slice(128 * half, 128 * half + 128)
                low = [planes[0, k, y, z] for k in range(12)]
                held = None
                for i in range(count + 1):
                    high = [planes[i + 1, k, y, z] for k in range(12)]
                    e = weight[lead + i, y, z]
                    f = mode_forces(element_modes(low, high))
                    done = {}
                    f = {key: done.setdefault(id(val), val * e) for key, val in f.items()}
                    now = []
                    for comp in range(3):
                        for q in range(2):
                            for r in range(2):
                                k = 4 * comp + 2 * q + r
                                slope = f[comp, 1, q, r]
                                level = f.get((comp, 0, q, r))
                                below = -slope if level is None else level - slope
                                above = slope if level is None else level + slope
                                if held is not None:
                                    layers[i - 1, k, y, z] = held[k] + below
                                now.append(above)
                    held = now
                    low = high
            return 0

        lax.fori_loop(0, NY // 8, column, 0)

        def to_nodes(i, _):
            inv = inverse[lead + i]
            for comp in range(3):
                across = []
                for r in range(2):
                    level, slope = layers[i, 4 * comp + r], layers[i, 4 * comp + 2 + r]
                    across.append((level - slope) + prev_y(level + slope, y_first))
                level, slope = across
                force = (level - slope) + prev_z(level + slope, z_first)
                target[comp, i] = inv * force - source[comp, i + 1]
            return 0

        lax.fori_loop(0, count, to_nodes, 0)

    shifted_operator(w0, w1, 6, 1)
    shifted_operator(w1, w2, 4, 2)

    totals = [jnp.zeros((8, 128), jnp.float32) for _ in range(6)]
    shifted_operator(w2, basis.at[2], 2, 3)
    for i in range(2):
        m = mass[3 + i]
        for comp in range(3):
            v = (w0[comp, 3 + i], w1[comp, 2 + i], w2[comp, 1 + i], basis[2, comp, i])
            mv = [m * a for a in v[:3]]
            products = (mv[0] * v[0], mv[0] * v[1], mv[1] * v[1], mv[1] * v[2], mv[2] * v[2], mv[2] * v[3])
            for k, product in enumerate(products):
                part = product[:, :128] + product[:, 128:]
                totals[k] = totals[k] + ((part[0:8] + part[8:16]) + (part[16:24] + part[24:32]))
    for k in range(6):
        moments[k : k + 1, :] = jnp.sum(totals[k], axis=0, keepdims=True)
    moments[6:8, :] = jnp.zeros((2, 128), jnp.float32)
    basis[0] = w0[:, 3:6]
    basis[1] = w1[:, 2:5]
    basis[2] = w2[:, 1:4]


def step_sizes(nu):
    eta = [nu[k] + nu[k + 1] for k in range(5)]

    def form(v, values):
        summed = None
        for i in range(len(v)):
            for j in range(i, len(v)):
                term = (v[i] * v[j]) * values[i + j]
                term = term if i == j else 2.0 * term
                summed = term if summed is None else summed + term
        return summed

    first = nu[0] / eta[0]
    z = [1.0 - first, -first]
    now = form(z, nu)
    beta = now / nu[0]
    p = [z[0] + beta, z[1]]
    second = now / form(p, eta)
    last = [z[0] - second * p[0], z[1] - second * (p[0] + p[1]), -(second * p[1])]
    then = form(last, nu)
    beta = then / now
    q = [last[0] + beta * p[0], last[1] + beta * p[1], last[2]]
    third = then / form(q, eta)
    return [first + second * p[0] + third * q[0], second * p[1] + third * q[1], third * q[2]]


def combine_kernel(parts, basis, displacement, energies, upper, planes, energy):
    y_first, y_last, z_first, z_last = plane_edges()
    total = parts[0]
    for i in range(1, 16):
        total = total + parts[i]
    nu = [jnp.sum(total[k : k + 1, :], axis=1, keepdims=True) for k in range(6)]
    coefficient = step_sizes(nu)
    wide = [jnp.broadcast_to(c, (NY, NZ)) for c in coefficient]
    for comp in range(3):
        for i in range(3):
            u = wide[0] * basis[0, comp, i] + wide[1] * basis[1, comp, i] + wide[2] * basis[2, comp, i]
            if i < 2:
                displacement[comp, i] = u
            for k, part in enumerate(plane_modes(u, y_last, z_last)):
                planes[i, 4 * comp + k] = part

    def column(tile, _):
        y = pl.ds(pl.multiple_of(tile * 8, 8), 8)
        for half in range(NZ // 128):
            z = slice(128 * half, 128 * half + 128)
            low = [planes[0, k, y, z] for k in range(12)]
            for i in range(2):
                high = [planes[i + 1, k, y, z] for k in range(12)]
                energy[i, y, z] = MODE_SCALE * mode_energy(element_modes(low, high))
                low = high
        return 0

    lax.fori_loop(0, NY // 8, column, 0)
    for load in range(LOADS):
        energies[load] = energy[:, 2 * load : 2 * load + 2, :]


def shards(density, fixed_mask, patch_index, patch_force):
    slab = lax.axis_index("space")
    load = lax.axis_index("load")
    code = jnp.where(fixed_mask == 0, patch_index, int(OUTSIDE)).astype(jnp.float32)
    mine = lax.dynamic_slice_in_dim(code, 2 * load, 2, axis=1)
    own = jnp.stack([density, mine])
    column = lax.all_to_all(jnp.broadcast_to(own[None], (16,) + own.shape), "space", 0, 0, tiled=True)
    rho = jnp.pad(column[:, 0].reshape(NX, 2, NZ), ((4, 4), (0, 0), (0, 0)))
    codes = jnp.pad(column[:, 1].reshape(NX, 2, NZ), ((4, 4), (0, 0), (0, 0)), constant_values=OUTSIDE)
    window = jnp.concatenate(
        [
            lax.dynamic_slice_in_dim(rho, 2 * slab, 9, axis=0),
            lax.dynamic_slice_in_dim(codes, 2 * slab + 1, 8, axis=0),
        ]
    )
    gathered = lax.all_to_all(jnp.broadcast_to(window[None], (16,) + window.shape), "load", 0, 0, tiled=True)

    vmem = pl.BlockSpec(memory_space=pltpu.VMEM)
    smem = pl.BlockSpec(memory_space=pltpu.SMEM)
    field = lambda *shape: pltpu.VMEM(shape + (NY, NZ), jnp.float32)
    basis, moments = pl.pallas_call(
        krylov_kernel,
        out_shape=(
            jax.ShapeDtypeStruct((3, 3, 3, NY, NZ), jnp.float32),
            jax.ShapeDtypeStruct((8, 128), jnp.float32),
        ),
        in_specs=[smem, smem, vmem],
        out_specs=(vmem, vmem),
        scratch_shapes=[field(17), field(9), field(8), field(8), field(3, 8), field(3, 6), field(3, 4), field(8, 12), field(6, 12)],
        name="krylov",
    )(slab.astype(jnp.int32).reshape(1), patch_force[0], gathered)
    parts = lax.all_to_all(jnp.broadcast_to(moments[None], (16, 8, 128)), "space", 0, 0, tiled=True)
    displacement, energies = pl.pallas_call(
        combine_kernel,
        out_shape=(
            jax.ShapeDtypeStruct((3, 2, NY, NZ), jnp.float32),
            jax.ShapeDtypeStruct((LOADS, 2, 2, NZ), jnp.float32),
        ),
        in_specs=[vmem, vmem],
        out_specs=(vmem, vmem),
        scratch_shapes=[field(1), field(3, 12), field(2)],
        name="combine",
    )(parts, basis)
    received = lax.all_to_all(energies, "load", 0, 0, tiled=True)
    summed = jnp.sum(received, axis=0)
    sensitivity = -3.0 * (1.0 - void_stiffness) * density**2 * (summed / LOADS)
    return (displacement[None], sensitivity)


def solution(mesh):
    in_specs = (
        P("space", "load", None),
        P("space", None, None),
        P("space", None, None),
        P("load", None, None),
    )
    out_specs = (P("load", None, "space", None, None), P("space", "load", None))
    return jax.shard_map(shards, mesh=mesh, in_specs=in_specs, out_specs=out_specs, check_vma=False)
```

profile of v0, /device:TPU:1, one launch (start us, length us, event | category | flops | bytes accessed | tf_op | source)
XLA Modules:
  0.0 82.2 jit_solution(7280169600360654193)
XLA Ops:
  0.6 0.0 copy-start.1
  0.6 0.7 fusion.1
  1.4 0.0 copy-done.1
  1.4 0.7 broadcast_in_dim.13
  2.1 7.3 %all-to-all-start = ((f32[16,2,2,2,256]{4,3,2,1,0:T(2,128)}), f32[16,2,2,2,256]{4,3,2,1,0:T(2,128)S(1)}, u32[]{:S(2)}, u32[]{:S(2)}) async-start(f32[16,2,2,2,256]{4,3,2,1,0:T(2,128)} %broadcast_in_dim.13), calls=%async_computation | async-start | bytes 262144 | tf_op jit(solution)/shard_map/all_to_all | solution.py:301
  9.4 6.1 %all-to-all-done = f32[16,2,2,2,256]{4,3,2,1,0:T(2,128)S(1)} async-done(((f32[16,2,2,2,256]{4,3,2,1,0:T(2,128)}), f32[16,2,2,2,256]{4,3,2,1,0:T(2,128)S(1)}, u32[]{:S(2)}, u32[]{:S(2)}) %all-to-all-start) | async-done | bytes 131104 | tf_op jit(solution)/shard_map/all_to_all | solution.py:301
  15.7 1.0 %broadcast_in_dim.14 = f32[16,17,2,256]{3,2,1,0:T(2,128)} broadcast(f32[17,2,256]{2,1,0:T(2,128)S(1)} %pad_maximum_fusion), dimensions={1,2,3} | broadcast | bytes 591872 | tf_op jit(solution)/shard_map/broadcast_in_dim | solution.py:310
  16.6 0.0 copy-start.2
  16.6 10.0 %all-to-all-start.1 = ((f32[16,17,2,256]{3,2,1,0:T(2,128)}), f32[16,17,2,256]{3,2,1,0:T(2,128)S(1)}, u32[]{:S(2)}, u32[]{:S(2)}) async-start(f32[16,17,2,256]{3,2,1,0:T(2,128)} %broadcast_in_dim.14), calls=%async_computation.1 | async-start | bytes 1114112 | tf_op jit(solution)/shard_map/all_to_all | solution.py:310
  26.6 0.0 copy-done.2
  26.6 0.6 copy.8
  27.2 17.4 %all-to-all-done.1.gathered = f32[16,17,2,256]{3,2,1,0:T(2,128)S(1)} async-done(((f32[16,17,2,256]{3,2,1,0:T(2,128)}), f32[16,17,2,256]{3,2,1,0:T(2,128)S(1)}, u32[]{:S(2)}, u32[]{:S(2)}) %all-to-all-start.1) | async-done | bytes 557088 | tf_op jit(solution)/shard_map/all_to_all | solution.py:310
  44.6 0.0 copy-start
  44.6 0.8 %copy-done = f32[16,17,2,256]{3,2,1,0:T(2,128)} copy-done((f32[16,17,2,256]{3,2,1,0:T(2,128)}, f32[16,17,2,256]{3,2,1,0:T(2,128)S(1)}, u32[]{:S(2)}) %copy-start) | copy-done | bytes 557080
  45.4 8.8 %krylov.1 = (f32[3,3,3,32,256]{4,3,2,1,0:T(8,128)}, f32[8,128]{1,0:T(8,128)}) custom-call(s32[1]{0:T(128)} %bitcast.slab, f32[3,16]{1,0:T(4,128)} %bitcast.13, f32[16,17,2,256]{3,2,1,0:T(2,128)} %copy-done), custom_call_target="tpu_custom_call" | custom-call | tf_op jit(solution)/shard_map/krylov/pallas_call | solution.py:315
  54.2 0.7 broadcast_in_dim.28
  54.9 11.5 %all_to_all.20.parts = f32[16,8,128]{2,1,0:T(8,128)} all-to-all(f32[16,8,128]{2,1,0:T(8,128)S(1)} %broadcast_in_dim.28), channel_id=1, replica_groups=mesh['load'=16,'space'=16] {'space'}, dimensions={0} | all-to-all | bytes 131072 | tf_op jit(solution)/shard_map/all_to_all | solution.py:326
  66.4 2.5 %combine.1 = (f32[3,2,32,256]{3,2,1,0:T(8,128)}, f32[16,2,2,256]{3,2,1,0:T(2,128)}) custom-call(f32[16,8,128]{2,1,0:T(8,128)} %all_to_all.20.parts, f32[3,3,3,32,256]{4,3,2,1,0:T(8,128)} %get-tuple-element.7.basis), custom_call_target="tpu_custom_call" | custom-call | tf_op jit(solution)/shard_map/combine/pallas_call | solution.py:327
  68.9 12.7 %all_to_all.21 = f32[16,2,2,256]{3,2,1,0:T(2,128)S(1)} all-to-all(f32[16,2,2,256]{3,2,1,0:T(2,128)} %get-tuple-element.9), channel_id=1, replica_groups=mesh['load'=16,'space'=16] {'load'}, dimensions={0} | all-to-all | bytes 131072 | tf_op jit(solution)/shard_map/all_to_all | solution.py:338
  81.6 0.6 multiply_multiply_fusion
  (6 shorter events, 0.1 us)
Async XLA Ops:
  0.6 0.8 copy-start.1
  2.1 13.4 %all-to-all-start = ((f32[16,2,2,2,256]{4,3,2,1,0:T(2,128)}), f32[16,2,2,2,256]{4,3,2,1,0:T(2,128)S(1)}, u32[]{:S(2)}, u32[]{:S(2)}) async-start(f32[16,2,2,2,256]{4,3,2,1,0:T(2,128)} %broadcast_in_dim.13), calls=%async_computation | async-start | bytes 262144 | tf_op jit(solution)/shard_map/all_to_all | solution.py:301
  16.6 10.0 %copy-start.2 = (f32[1,3,16]{2,0,1:T(1,128)S(1)}, f32[1,3,16]{2,0,1:T(1,128)}, u32[]{:S(2)}) copy-start(f32[1,3,16]{2,0,1:T(1,128)} %param.7) | copy-start | bytes 580
  16.6 28.0 %all-to-all-start.1 = ((f32[16,17,2,256]{3,2,1,0:T(2,128)}), f32[16,17,2,256]{3,2,1,0:T(2,128)S(1)}, u32[]{:S(2)}, u32[]{:S(2)}) async-start(f32[16,17,2,256]{3,2,1,0:T(2,128)} %broadcast_in_dim.14), calls=%async_computation.1 | async-start | bytes 1114112 | tf_op jit(solution)/shard_map/all_to_all | solution.py:310
  44.6 0.8 %copy-start = (f32[16,17,2,256]{3,2,1,0:T(2,128)}, f32[16,17,2,256]{3,2,1,0:T(2,128)S(1)}, u32[]{:S(2)}) copy-start(f32[16,17,2,256]{3,2,1,0:T(2,128)S(1)} %all-to-all-done.1.gathered) | copy-start | bytes 1671172
where the time goes:
time: 82.7 us; the launch traced here: 82.2 us
  blocking collectives  24.2 us (29%)
  waiting for transfers between devices  23.5 us (28%)
  starting transfers between devices  17.3 us (21%)
  Pallas kernels  11.2 us (14%)
  local copies, waits for them, and re-layouts  3.82 us (5%)
  other arithmetic  1.41 us (2%)
    all_to_all x1, waiting for transfers between devices, shards(): lax.all_to_all(jnp.broadcast_to(window[None], (16,) + window.shape), 'loa...  17.4 us
    all_to_all x1, blocking collectives, shards(): received = lax.all_to_all(energies, 'load', 0, 0, tiled=True)  12.7 us
    all_to_all x1, blocking collectives, shards(): lax.all_to_all(jnp.broadcast_to(moments[None], (16, 8, 128)), 'space', 0,...  11.5 us
    all_to_all x1, starting transfers between devices, shards(): lax.all_to_all(jnp.broadcast_to(window[None], (16,) + window.shape), 'loa...  9.98 us
    pallas_call x1, Pallas kernels, shards(): pl.pallas_call(krylov_kernel, out_shape=(jax.ShapeDtypeStruct((3, 3, 3, N...  8.75 us
    all_to_all x1, starting transfers between devices, shards(): lax.all_to_all(jnp.broadcast_to(own[None], (16,) + own.shape), 'space', 0...  7.33 us
    all_to_all x1, waiting for transfers between devices, shards(): lax.all_to_all(jnp.broadcast_to(own[None], (16,) + own.shape), 'space', 0...  6.11 us
    pallas_call x1, Pallas kernels, shards(): pl.pallas_call(combine_kernel, out_shape=(jax.ShapeDtypeStruct((3, 2, NY,...  2.49 us
  transfers between devices with their start and end apart: 2, of which 2 were waited for; matrix products, arithmetic and copies ran while one was open for 1% of the time, Pallas kernels for 0%

commit v1 on v0

--- a/solution.py
+++ b/solution.py
@@ -125,12 +125,17 @@
     return summed + (SHEAR / 3.0) * triple + DIAGONAL * corner
 
 
-def krylov_kernel(slab, table, gathered, basis, moments, rows, weight, inverse, mass, w0, w1, w2, planes, layers):
-    first = 2 * slab[0] - 3
+def krylov_kernel(place, table, codes, *refs):
+    pieces, (basis, moments, staged, rows, weight, inverse, mass, w0, w1, planes, layers) = refs[:4], refs[4:]
+    own = place[1]
+    first = 2 * place[0] - 2
     y_first, y_last, z_first, z_last = plane_edges()
 
+    for far in range(4):
+        for near in range(4):
+            staged[own ^ (4 * far + near)] = pieces[far][near]
     for load in range(LOADS):
-        rows[:, 2 * load : 2 * load + 2, :] = gathered[load]
+        rows[:, 2 * load : 2 * load + 2, :] = staged[load]
 
     def set_weight(i, _):
         layer = first - 1 + i
@@ -139,34 +144,38 @@
         weight[i] = (MODE_SCALE * inside) * (void_stiffness + (1.0 - void_stiffness) * (rho * rho * rho))
         return 0
 
-    lax.fori_loop(0, 9, set_weight, 0)
-
-    def set_plane(i, _):
+    lax.fori_loop(0, 8, set_weight, 0)
+
+    def set_plane(i, code):
         both_layers = weight[i] + weight[i + 1]
         across = both_layers + prev_y(both_layers, y_first)
         diag = (DIAGONAL / MODE_SCALE) * (across + prev_z(across, z_first))
-        code = rows[9 + i]
         inv = jnp.where(code < OUTSIDE - 0.5, 1.0 / diag, 0.0)
         inverse[i] = inv
         mass[i] = diag
         scaled = inv * (1.0 + 2.0 * (first + i).astype(jnp.float32) / (NX - 1))
+        force = [jnp.zeros((NY, NZ), jnp.float32) for _ in range(3)]
+        for patch in range(PATCHES):
+            here = code == float(patch)
+            force = [jnp.where(here, table[comp, patch], force[comp]) for comp in range(3)]
         for comp in range(3):
-            force = jnp.zeros((NY, NZ), jnp.float32)
-            for patch in range(PATCHES):
-                force = jnp.where(code == float(patch), table[comp, patch], force)
-            w0[comp, i] = scaled * force
-        return 0
-
-    lax.fori_loop(0, 8, set_plane, 0)
-
-    def shifted_operator(source, target, count, lead):
-        def to_modes(i, _):
+            w0[comp, i] = scaled * force[comp]
+
+    lax.fori_loop(0, 2, lambda i, _: (set_plane(i, rows[8 + i]), 0)[1], 0)
+    lax.fori_loop(2, 4, lambda i, _: (set_plane(i, codes[i - 2]), 0)[1], 0)
+    lax.fori_loop(4, 7, lambda i, _: (set_plane(i, rows[6 + i]), 0)[1], 0)
+
+    def to_modes(source, count):
+        def body(i, _):
             for comp in range(3):
                 for k, part in enumerate(plane_modes(source[comp, i], y_last, z_last)):
                     planes[i, 4 * comp + k] = part
             return 0
 
-        lax.fori_loop(0, count + 2, to_modes, 0)
+        lax.fori_loop(0, count, body, 0)
+
+    def shifted_operator(source, target, count, lead):
+        to_modes(source, count + 2)
 
         def column(tile, _):
             y = pl.ds(pl.multiple_of(tile * 8, 8), 8)
@@ -212,30 +221,43 @@
 
         lax.fori_loop(0, count, to_nodes, 0)
 
-    shifted_operator(w0, w1, 6, 1)
-    shifted_operator(w1, w2, 4, 2)
-
-    totals = [jnp.zeros((8, 128), jnp.float32) for _ in range(6)]
-    shifted_operator(w2, basis.at[2], 2, 3)
+    shifted_operator(w0, w1, 5, 1)
+    shifted_operator(w1, basis.at[2], 3, 2)
+    basis[0] = w0[:, 2:5]
+    basis[1] = w1[:, 1:4]
+
+    to_modes(basis.at[2], 3)
+
+    def column(tile, summed):
+        y = pl.ds(pl.multiple_of(tile * 8, 8), 8)
+        for half in range(NZ // 128):
+            z = slice(128 * half, 128 * half + 128)
+            low = [planes[0, k, y, z] for k in range(12)]
+            for i in range(2):
+                high = [planes[i + 1, k, y, z] for k in range(12)]
+                summed = summed + weight[3 + i, y, z] * mode_energy(element_modes(low, high))
+                low = high
+        return summed
+
+    totals = [jnp.zeros((8, 128), jnp.float32) for _ in range(5)]
+    totals.append(lax.fori_loop(0, NY // 8, column, jnp.zeros((8, 128), jnp.float32)))
     for i in range(2):
-        m = mass[3 + i]
+        m = mass[2 + i]
         for comp in range(3):
-            v = (w0[comp, 3 + i], w1[comp, 2 + i], w2[comp, 1 + i], basis[2, comp, i])
-            mv = [m * a for a in v[:3]]
-            products = (mv[0] * v[0], mv[0] * v[1], mv[1] * v[1], mv[1] * v[2], mv[2] * v[2], mv[2] * v[3])
+            v = [basis[k, comp, i] for k in range(3)]
+            mv = [m * a for a in v]
+            products = (mv[0] * v[0], mv[0] * v[1], mv[1] * v[1], mv[1] * v[2], mv[2] * v[2])
             for k, product in enumerate(products):
                 part = product[:, :128] + product[:, 128:]
                 totals[k] = totals[k] + ((part[0:8] + part[8:16]) + (part[16:24] + part[24:32]))
-    for k in range(6):
-        moments[k : k + 1, :] = jnp.sum(totals[k], axis=0, keepdims=True)
-    moments[6:8, :] = jnp.zeros((2, 128), jnp.float32)
-    basis[0] = w0[:, 3:6]
-    basis[1] = w1[:, 2:5]
-    basis[2] = w2[:, 1:4]
+    sums = [jnp.sum(total, axis=0, keepdims=True) for total in totals]
+    block = jnp.concatenate(sums + [jnp.zeros((2, 128), jnp.float32)], axis=0)
+    for i in range(16):
+        moments[i] = block
 
 
 def step_sizes(nu):
-    eta = [nu[k] + nu[k + 1] for k in range(5)]
+    eta = [nu[k] + nu[k + 1] for k in range(4)] + [nu[5]]
 
     def form(v, values):
         summed = None
@@ -260,7 +282,7 @@
     return [first + second * p[0] + third * q[0], second * p[1] + third * q[1], third * q[2]]
 
 
-def combine_kernel(parts, basis, displacement, energies, upper, planes, energy):
+def combine_kernel(parts, basis, displacement, energies, planes, energy):
     y_first, y_last, z_first, z_last = plane_edges()
     total = parts[0]
     for i in range(1, 16):
@@ -292,6 +314,10 @@
         energies[load] = energy[:, 2 * load : 2 * load + 2, :]
 
 
+def others(x, distance):
+    return [lax.ppermute(x, "load", [(i, i ^ (k * distance)) for i in range(LOADS)]) for k in range(1, 4)]
+
+
 def shards(density, fixed_mask, patch_index, patch_force):
     slab = lax.axis_index("space")
     load = lax.axis_index("load")
@@ -299,15 +325,12 @@
     mine = lax.dynamic_slice_in_dim(code, 2 * load, 2, axis=1)
     own = jnp.stack([density, mine])
     column = lax.all_to_all(jnp.broadcast_to(own[None], (16,) + own.shape), "space", 0, 0, tiled=True)
-    rho = jnp.pad(column[:, 0].reshape(NX, 2, NZ), ((4, 4), (0, 0), (0, 0)))
-    codes = jnp.pad(column[:, 1].reshape(NX, 2, NZ), ((4, 4), (0, 0), (0, 0)), constant_values=OUTSIDE)
-    window = jnp.concatenate(
-        [
-            lax.dynamic_slice_in_dim(rho, 2 * slab, 9, axis=0),
-            lax.dynamic_slice_in_dim(codes, 2 * slab + 1, 8, axis=0),
-        ]
-    )
-    gathered = lax.all_to_all(jnp.broadcast_to(window[None], (16,) + window.shape), "load", 0, 0, tiled=True)
+    rho = jnp.pad(column[:, 0].reshape(NX, 2, NZ), ((3, 3), (0, 0), (0, 0)))
+    codes = jnp.pad(column[:, 1].reshape(NX, 2, NZ), ((2, 3), (0, 0), (0, 0)), constant_values=OUTSIDE)
+    near = lax.dynamic_slice_in_dim(codes, 2 * slab, 7, axis=0)
+    window = jnp.concatenate([lax.dynamic_slice_in_dim(rho, 2 * slab, 8, axis=0), near[:2], near[4:]])
+    line = jnp.stack([window] + others(window, 1))
+    pieces = [line] + others(line, 4)
 
     vmem = pl.BlockSpec(memory_space=pltpu.VMEM)
     smem = pl.BlockSpec(memory_space=pltpu.SMEM)
@@ -316,14 +339,15 @@
         krylov_kernel,
         out_shape=(
             jax.ShapeDtypeStruct((3, 3, 3, NY, NZ), jnp.float32),
-            jax.ShapeDtypeStruct((8, 128), jnp.float32),
+            jax.ShapeDtypeStruct((16, 8, 128), jnp.float32),
         ),
-        in_specs=[smem, smem, vmem],
+        in_specs=[smem, smem, vmem] + [vmem] * 4,
         out_specs=(vmem, vmem),
-        scratch_shapes=[field(17), field(9), field(8), field(8), field(3, 8), field(3, 6), field(3, 4), field(8, 12), field(6, 12)],
+        scratch_shapes=[pltpu.VMEM((LOADS, 13, 2, NZ), jnp.float32)]
+        + [field(13), field(8), field(7), field(7), field(3, 7), field(3, 5), field(7, 12), field(5, 12)],
         name="krylov",
-    )(slab.astype(jnp.int32).reshape(1), patch_force[0], gathered)
-    parts = lax.all_to_all(jnp.broadcast_to(moments[None], (16, 8, 128)), "space", 0, 0, tiled=True)
+    )(jnp.stack([slab, load]).astype(jnp.int32), patch_force[0], code, *pieces)
+    parts = lax.all_to_all(moments, "space", 0, 0, tiled=True)
     displacement, energies = pl.pallas_call(
         combine_kernel,
         out_shape=(
@@ -332,7 +356,7 @@
         ),
         in_specs=[vmem, vmem],
         out_specs=(vmem, vmem),
-        scratch_shapes=[field(1), field(3, 12), field(2)],
+        scratch_shapes=[field(3, 12), field(2)],
         name="combine",
     )(parts, basis)
     received = lax.all_to_all(energies, "load", 0, 0, tiled=True)

time: 82.7 us -> 74.8 us (0.904)
  waiting for transfers between devices: 23.5 us -> 13.4 us
  blocking collectives: 24.2 us -> 26.9 us
  Pallas kernels: 11.2 us -> 9.7 us
  other arithmetic: 1.41 us -> 2.25 us
    all_to_all x1 -> x0, waiting for transfers between devices: 17.4 us -> none  [shards(): lax.all_to_all(jnp.broadcast_to(window[None], (16,) + window.shape), 'loa...]
    ppermute x0 -> x6, starting transfers between devices: none -> 10.6 us  [others(): lax.ppermute(x, 'load', [(i, i ^ k * distance) for i in range(LOADS)])]
    all_to_all x1 -> x0, starting transfers between devices: 9.98 us -> none  [shards(): lax.all_to_all(jnp.broadcast_to(window[None], (16,) + window.shape), 'loa...]
    ppermute x0 -> x6, waiting for transfers between devices: none -> 8.52 us  [others(): lax.ppermute(x, 'load', [(i, i ^ k * distance) for i in range(LOADS)])]
    all_to_all x1, blocking collectives: 11.5 us -> 13.5 us  [shards(): parts = lax.all_to_all(moments, 'space', 0, 0, tiled=True)]
    broadcast_in_dim x2 -> x0, local copies, waits for them, and re-layouts: 1.64 us -> none  [the longest x1 0.95 us: shards(): jnp.broadcast_to(window[None], (16,) + window.shape)]
    pallas_call x1, Pallas kernels: 8.75 us -> 7.21 us  [shards(): pl.pallas_call(krylov_kernel, out_shape=(jax.ShapeDtypeStruct((3, 3, 3, N...]
    all_to_all x1, waiting for transfers between devices: 6.11 us -> 4.85 us  [shards(): lax.all_to_all(jnp.broadcast_to(own[None], (16,) + own.shape), 'space', 0...]
  transfers between devices with their start and end apart: 2 -> 7, of which waited for: 2 -> 5; matrix products, arithmetic and copies ran while one was open for 1% -> 2% of each run, Pallas kernels for 0% -> 0%
where the time goes in v1:
time: 74.8 us; the launch traced here: 74.3 us
  blocking collectives  26.9 us (36%)
  starting transfers between devices  18 us (24%)
  waiting for transfers between devices  13.4 us (18%)
  Pallas kernels  9.7 us (13%)
  local copies, waits for them, and re-layouts  3.39 us (5%)
  other arithmetic  2.25 us (3%)
  between operations  0.75 us (1%)
    all_to_all x1, blocking collectives, shards(): parts = lax.all_to_all(moments, 'space', 0, 0, tiled=True)  13.5 us
    all_to_all x1, blocking collectives, shards(): received = lax.all_to_all(energies, 'load', 0, 0, tiled=True)  13.4 us
    ppermute x6, starting transfers between devices, others(): lax.ppermute(x, 'load', [(i, i ^ k * distance) for i in range(LOADS)])  10.6 us
    ppermute x6, waiting for transfers between devices, others(): lax.ppermute(x, 'load', [(i, i ^ k * distance) for i in range(LOADS)])  8.52 us
    all_to_all x1, starting transfers between devices, shards(): lax.all_to_all(jnp.broadcast_to(own[None], (16,) + own.shape), 'space', 0...  7.33 us
    pallas_call x1, Pallas kernels, shards(): pl.pallas_call(krylov_kernel, out_shape=(jax.ShapeDtypeStruct((3, 3, 3, N...  7.21 us
    all_to_all x1, waiting for transfers between devices, shards(): lax.all_to_all(jnp.broadcast_to(own[None], (16,) + own.shape), 'space', 0...  4.85 us
    unnamed x15, local copies, waits for them, and re-layouts  2.61 us
  transfers between devices with their start and end apart: 7, of which 5 were waited for; matrix products, arithmetic and copies ran while one was open for 2% of the time, Pallas kernels for 0%

profile of v1, /device:TPU:1, one launch (start us, length us, event | category | flops | bytes accessed | tf_op | source)
XLA Modules:
  0.0 74.3 jit_solution(17335415178189046285)
XLA Ops:
  0.6 0.9 %select_convert_fusion.codes = f32[2,32,256]{2,1,0:T(8,128)S(1)} fusion(s32[2,32,256]{2,1,0:T(8,128)} %param.6, s32[2,32,256]{2,1,0:T(8,128)} %param.5), kind=kLoop, calls=%fused_computation.2 | loop fusion | flops 49152 | bytes 196608 | tf_op jit(solution)/shard_map/convert_element_type | solution.py:324
  1.5 0.0 copy-start.1
  1.5 0.0 copy-start.5
  1.6 0.7 copy-done.5
  2.3 0.7 broadcast_in_dim.14
  2.9 0.0 copy-done.1
  2.9 7.3 %all-to-all-start = ((f32[16,2,2,2,256]{4,3,2,1,0:T(2,128)}), f32[16,2,2,2,256]{4,3,2,1,0:T(2,128)S(1)}, u32[]{:S(2)}, u32[]{:S(2)}) async-start(f32[16,2,2,2,256]{4,3,2,1,0:T(2,128)} %broadcast_in_dim.14), calls=%async_computation | async-start | bytes 262144 | tf_op jit(solution)/shard_map/all_to_all | solution.py:327
  10.3 0.0 copy-start.6
  10.3 0.7 copy-done.6
  11.0 0.6 copy.8
  11.5 4.9 %all-to-all-done = f32[16,2,2,2,256]{4,3,2,1,0:T(2,128)S(1)} async-done(((f32[16,2,2,2,256]{4,3,2,1,0:T(2,128)}), f32[16,2,2,2,256]{4,3,2,1,0:T(2,128)S(1)}, u32[]{:S(2)}, u32[]{:S(2)}) %all-to-all-start) | async-done | bytes 131104 | tf_op jit(solution)/shard_map/all_to_all | solution.py:327
  16.5 6.1 %collective-permute-start.1 = (f32[13,2,256]{2,1,0:T(2,128)S(1)}, f32[13,2,256]{2,1,0:T(2,128)S(1)}, u32[]{:S(2)}, u32[]{:S(2)}) collective-permute-start(f32[13,2,256]{2,1,0:T(2,128)S(1)} %pad_maximum_fusion.1), channel_id=1, source_target_pairs={{0,32},{16,48},{32,0},{48,16},{64,96},{80,112},{96,64},{112,80},{1... | collective-permute-start | bytes 79880 | tf_op jit(solution)/shard_map/ppermute | solution.py:318
  22.6 1.2 %collective-permute-start = (f32[13,2,256]{2,1,0:T(2,128)S(1)}, f32[13,2,256]{2,1,0:T(2,128)S(1)}, u32[]{:S(2)}, u32[]{:S(2)}) collective-permute-start(f32[13,2,256]{2,1,0:T(2,128)S(1)} %pad_maximum_fusion.1), channel_id=1, source_target_pairs={{0,16},{16,0},{32,48},{48,32},{64,80},{80,64},{96,112},{112,96},{1... | collective-permute-start | bytes 79880 | tf_op jit(solution)/shard_map/ppermute | solution.py:318
  23.8 0.0 collective-permute-start.2
  23.8 0.0 collective-permute-done.1
  23.8 2.9 %collective-permute-done = f32[13,2,256]{2,1,0:T(2,128)S(1)} collective-permute-done((f32[13,2,256]{2,1,0:T(2,128)S(1)}, f32[13,2,256]{2,1,0:T(2,128)S(1)}, u32[]{:S(2)}, u32[]{:S(2)}) %collective-permute-start) | collective-permute-done | bytes 26656 | tf_op jit(solution)/shard_map/ppermute | solution.py:318
  26.8 1.9 %collective-permute-done.2 = f32[13,2,256]{2,1,0:T(2,128)S(1)} collective-permute-done((f32[13,2,256]{2,1,0:T(2,128)S(1)}, f32[13,2,256]{2,1,0:T(2,128)S(1)}, u32[]{:S(2)}, u32[]{:S(2)}) %collective-permute-start.2) | collective-permute-done | bytes 26656 | tf_op jit(solution)/shard_map/ppermute | solution.py:318
  28.6 0.1 pad_maximum_fusion.refs_0_
  28.7 0.0 copy-start
  28.7 2.6 %collective-permute-start.5 = (f32[4,13,2,256]{3,2,1,0:T(2,128)S(1)}, f32[4,13,2,256]{3,2,1,0:T(2,128)S(1)}, u32[]{:S(2)}, u32[]{:S(2)}) collective-permute-start(f32[4,13,2,256]{3,2,1,0:T(2,128)S(1)} %pad_maximum_fusion.refs_0_), channel_id=1, source_target_pairs={{0,192},{16,208},{32,224},{48,240},{64,128},{80,144},{96,160},{112... | collective-permute-start | bytes 319496 | tf_op jit(solution)/shard_map/ppermute | solution.py:318
  31.2 0.5 collective-permute-start.4
  31.8 0.3 collective-permute-start.3
  32.0 0.6 pad_add_fusion.place
  32.7 1.4 %collective-permute-done.5.refs_3_ = f32[4,13,2,256]{3,2,1,0:T(2,128)S(1)} collective-permute-done((f32[4,13,2,256]{3,2,1,0:T(2,128)S(1)}, f32[4,13,2,256]{3,2,1,0:T(2,128)S(1)}, u32[]{:S(2)}, u32[]{:S(2)}) %collective-permute-start.5) | collective-permute-done | bytes 106528 | tf_op jit(solution)/shard_map/ppermute | solution.py:318
  34.0 0.0 copy-start.2
  34.0 2.4 %collective-permute-done.4.refs_2_ = f32[4,13,2,256]{3,2,1,0:T(2,128)S(1)} collective-permute-done((f32[4,13,2,256]{3,2,1,0:T(2,128)S(1)}, f32[4,13,2,256]{3,2,1,0:T(2,128)S(1)}, u32[]{:S(2)}, u32[]{:S(2)}) %collective-permute-start.4) | collective-permute-done | bytes 106528 | tf_op jit(solution)/shard_map/ppermute | solution.py:318
  36.4 0.0 copy-start.3
  36.4 0.0 collective-permute-done.3.refs_1_
  36.4 0.0 copy-start.4
  36.4 0.0 copy-done
  36.4 0.0 copy-done.2
  36.4 0.6 copy-done.3
  37.0 0.1 copy-done.4
  37.1 7.2 %krylov.1 = (f32[3,3,3,32,256]{4,3,2,1,0:T(8,128)}, f32[16,8,128]{2,1,0:T(8,128)}) custom-call(s32[2]{0:T(128)} %pad_add_fusion.place, f32[3,16]{1,0:T(4,128)} %bitcast.23, f32[2,32,256]{2,1,0:T(8,128)} %copy-done.1, f32[4,13,2,256]{3,2,1,0:T(2,128)} %copy-done, f32[4,13,2,256]{3,2,1,0:T(2,128)} %copy-done.4, f32[4,13,2,256]{3,2,1,0:T(2,128)} %copy-done.3, ...), custom_call_target="tpu_custom_call" | custom-call | tf_op jit(solution)/shard_map/krylov/pallas_call | solution.py:338
  44.3 13.5 %all_to_all.15.parts = f32[16,8,128]{2,1,0:T(8,128)} all-to-all(f32[16,8,128]{2,1,0:T(8,128)} %get-tuple-element.6), channel_id=1, replica_groups=mesh['load'=16,'space'=16] {'space'}, dimensions={0} | all-to-all | bytes 131072 | tf_op jit(solution)/shard_map/all_to_all | solution.py:350
  57.8 2.5 %combine.1 = (f32[3,2,32,256]{3,2,1,0:T(8,128)}, f32[16,2,2,256]{3,2,1,0:T(2,128)}) custom-call(f32[16,8,128]{2,1,0:T(8,128)} %all_to_all.15.parts, f32[3,3,3,32,256]{4,3,2,1,0:T(8,128)} %get-tuple-element.7.basis), custom_call_target="tpu_custom_call" | custom-call | tf_op jit(solution)/shard_map/combine/pallas_call | solution.py:351
  60.3 13.4 %all_to_all.16 = f32[16,2,2,256]{3,2,1,0:T(2,128)S(1)} all-to-all(f32[16,2,2,256]{3,2,1,0:T(2,128)} %get-tuple-element.9), channel_id=1, replica_groups=mesh['load'=16,'space'=16] {'load'}, dimensions={0} | all-to-all | bytes 131072 | tf_op jit(solution)/shard_map/all_to_all | solution.py:362
  73.7 0.6 multiply_multiply_fusion
  (9 shorter events, 0.2 us)
Async XLA Ops:
  1.5 1.4 %copy-start.1 = (f32[2,32,256]{2,1,0:T(8,128)}, f32[2,32,256]{2,1,0:T(8,128)S(1)}, u32[]{:S(2)}) copy-start(f32[2,32,256]{2,1,0:T(8,128)S(1)} %select_convert_fusion.codes) | copy-start | bytes 196612
  1.5 0.7 copy-start.5
  2.9 13.4 %all-to-all-start = ((f32[16,2,2,2,256]{4,3,2,1,0:T(2,128)}), f32[16,2,2,2,256]{4,3,2,1,0:T(2,128)S(1)}, u32[]{:S(2)}, u32[]{:S(2)}) async-start(f32[16,2,2,2,256]{4,3,2,1,0:T(2,128)} %broadcast_in_dim.14), calls=%async_computation | async-start | bytes 262144 | tf_op jit(solution)/shard_map/all_to_all | solution.py:327
  10.3 0.7 copy-start.6
  16.5 7.3 %collective-permute-start.1 = (f32[13,2,256]{2,1,0:T(2,128)S(1)}, f32[13,2,256]{2,1,0:T(2,128)S(1)}, u32[]{:S(2)}, u32[]{:S(2)}) collective-permute-start(f32[13,2,256]{2,1,0:T(2,128)S(1)} %pad_maximum_fusion.1), channel_id=1, source_target_pairs={{0,32},{16,48},{32,0},{48,16},{64,96},{80,112},{96,64},{112,80},{1... | collective-permute-start | bytes 79880 | tf_op jit(solution)/shard_map/ppermute | solution.py:318
  22.6 4.1 %collective-permute-start = (f32[13,2,256]{2,1,0:T(2,128)S(1)}, f32[13,2,256]{2,1,0:T(2,128)S(1)}, u32[]{:S(2)}, u32[]{:S(2)}) collective-permute-start(f32[13,2,256]{2,1,0:T(2,128)S(1)} %pad_maximum_fusion.1), channel_id=1, source_target_pairs={{0,16},{16,0},{32,48},{48,32},{64,80},{80,64},{96,112},{112,96},{1... | collective-permute-start | bytes 79880 | tf_op jit(solution)/shard_map/ppermute | solution.py:318
  23.8 4.8 %collective-permute-start.2 = (f32[13,2,256]{2,1,0:T(2,128)S(1)}, f32[13,2,256]{2,1,0:T(2,128)S(1)}, u32[]{:S(2)}, u32[]{:S(2)}) collective-permute-start(f32[13,2,256]{2,1,0:T(2,128)S(1)} %pad_maximum_fusion.1), channel_id=1, source_target_pairs={{0,48},{16,32},{32,16},{48,0},{64,112},{80,96},{96,80},{112,64},{1... | collective-permute-start | bytes 79880 | tf_op jit(solution)/shard_map/ppermute | solution.py:318
  28.7 7.7 %copy-start = (f32[4,13,2,256]{3,2,1,0:T(2,128)}, f32[4,13,2,256]{3,2,1,0:T(2,128)S(1)}, u32[]{:S(2)}) copy-start(f32[4,13,2,256]{3,2,1,0:T(2,128)S(1)} %pad_maximum_fusion.refs_0_) | copy-start | bytes 319492
  28.7 5.4 %collective-permute-start.5 = (f32[4,13,2,256]{3,2,1,0:T(2,128)S(1)}, f32[4,13,2,256]{3,2,1,0:T(2,128)S(1)}, u32[]{:S(2)}, u32[]{:S(2)}) collective-permute-start(f32[4,13,2,256]{3,2,1,0:T(2,128)S(1)} %pad_maximum_fusion.refs_0_), channel_id=1, source_target_pairs={{0,192},{16,208},{32,224},{48,240},{64,128},{80,144},{96,160},{112... | collective-permute-start | bytes 319496 | tf_op jit(solution)/shard_map/ppermute | solution.py:318
  31.2 5.2 %collective-permute-start.4 = (f32[4,13,2,256]{3,2,1,0:T(2,128)S(1)}, f32[4,13,2,256]{3,2,1,0:T(2,128)S(1)}, u32[]{:S(2)}, u32[]{:S(2)}) collective-permute-start(f32[4,13,2,256]{3,2,1,0:T(2,128)S(1)} %pad_maximum_fusion.refs_0_), channel_id=1, source_target_pairs={{0,128},{16,144},{32,160},{48,176},{64,192},{80,208},{96,224},{112... | collective-permute-start | bytes 319496 | tf_op jit(solution)/shard_map/ppermute | solution.py:318
  31.8 4.6 %collective-permute-start.3 = (f32[4,13,2,256]{3,2,1,0:T(2,128)S(1)}, f32[4,13,2,256]{3,2,1,0:T(2,128)S(1)}, u32[]{:S(2)}, u32[]{:S(2)}) collective-permute-start(f32[4,13,2,256]{3,2,1,0:T(2,128)S(1)} %pad_maximum_fusion.refs_0_), channel_id=1, source_target_pairs={{0,64},{16,80},{32,96},{48,112},{64,0},{80,16},{96,32},{112,48},{1... | collective-permute-start | bytes 319496 | tf_op jit(solution)/shard_map/ppermute | solution.py:318
  34.0 2.4 %copy-start.2 = (f32[4,13,2,256]{3,2,1,0:T(2,128)}, f32[4,13,2,256]{3,2,1,0:T(2,128)S(1)}, u32[]{:S(2)}) copy-start(f32[4,13,2,256]{3,2,1,0:T(2,128)S(1)} %collective-permute-done.5.refs_3_) | copy-start | bytes 319492
  36.4 0.6 copy-start.3
  36.4 0.7 copy-start.4

commit v2 on v1

--- a/solution.py
+++ b/solution.py
@@ -8,7 +8,6 @@
 NX, NY, NZ = 32, 32, 256
 PATCHES = 16
 LOADS = 16
-OUTSIDE = 16.0
 void_stiffness = 0.001
 poisson_ratio = 0.3
 LAME = poisson_ratio / ((1.0 + poisson_ratio) * (1.0 - 2.0 * poisson_ratio))
@@ -125,7 +124,7 @@
     return summed + (SHEAR / 3.0) * triple + DIAGONAL * corner
 
 
-def krylov_kernel(place, table, codes, *refs):
+def krylov_kernel(place, table, fixed, patches, *refs):
     pieces, (basis, moments, staged, rows, weight, inverse, mass, w0, w1, planes, layers) = refs[:4], refs[4:]
     own = place[1]
     first = 2 * place[0] - 2
@@ -150,19 +149,19 @@
         both_layers = weight[i] + weight[i + 1]
         across = both_layers + prev_y(both_layers, y_first)
         diag = (DIAGONAL / MODE_SCALE) * (across + prev_z(across, z_first))
-        inv = jnp.where(code < OUTSIDE - 0.5, 1.0 / diag, 0.0)
+        inv = jnp.where(code > 0.5, 1.0 / diag, 0.0)
         inverse[i] = inv
         mass[i] = diag
         scaled = inv * (1.0 + 2.0 * (first + i).astype(jnp.float32) / (NX - 1))
         force = [jnp.zeros((NY, NZ), jnp.float32) for _ in range(3)]
         for patch in range(PATCHES):
-            here = code == float(patch)
+            here = code == float(patch + 1)
             force = [jnp.where(here, table[comp, patch], force[comp]) for comp in range(3)]
         for comp in range(3):
             w0[comp, i] = scaled * force[comp]
 
     lax.fori_loop(0, 2, lambda i, _: (set_plane(i, rows[8 + i]), 0)[1], 0)
-    lax.fori_loop(2, 4, lambda i, _: (set_plane(i, codes[i - 2]), 0)[1], 0)
+    lax.fori_loop(2, 4, lambda i, _: (set_plane(i, jnp.where(fixed[i - 2] == 0, patches[i - 2] + 1, 0).astype(jnp.float32)), 0)[1], 0)
     lax.fori_loop(4, 7, lambda i, _: (set_plane(i, rows[6 + i]), 0)[1], 0)
 
     def to_modes(source, count):
@@ -321,14 +320,18 @@
 def shards(density, fixed_mask, patch_index, patch_force):
     slab = lax.axis_index("space")
     load = lax.axis_index("load")
-    code = jnp.where(fixed_mask == 0, patch_index, int(OUTSIDE)).astype(jnp.float32)
-    mine = lax.dynamic_slice_in_dim(code, 2 * load, 2, axis=1)
-    own = jnp.stack([density, mine])
-    column = lax.all_to_all(jnp.broadcast_to(own[None], (16,) + own.shape), "space", 0, 0, tiled=True)
-    rho = jnp.pad(column[:, 0].reshape(NX, 2, NZ), ((3, 3), (0, 0), (0, 0)))
-    codes = jnp.pad(column[:, 1].reshape(NX, 2, NZ), ((2, 3), (0, 0), (0, 0)), constant_values=OUTSIDE)
-    near = lax.dynamic_slice_in_dim(codes, 2 * slab, 7, axis=0)
-    window = jnp.concatenate([lax.dynamic_slice_in_dim(rho, 2 * slab, 8, axis=0), near[:2], near[4:]])
+    core = slab % 2
+    fixed_rows = lax.dynamic_slice_in_dim(fixed_mask, 2 * load, 2, axis=1)
+    patch_rows = lax.dynamic_slice_in_dim(patch_index, 2 * load, 2, axis=1)
+    mine = jnp.where(fixed_rows == 0, patch_rows + 1, 0).astype(jnp.float32)
+    own = jnp.stack([density, mine], 1)
+    partner = lax.ppermute(own, "space", [(i, i ^ 1) for i in range(16)])
+    chip = jnp.concatenate([jnp.where(core == 0, own, partner), jnp.where(core == 0, partner, own)])
+    below = lax.ppermute(chip, "space", [(i, i + 2) for i in range(14)])
+    above = lax.ppermute(chip, "space", [(i + 2, i) for i in range(14)])
+    lane = jnp.concatenate([below, chip, above])
+    lane = lax.dynamic_slice_in_dim(lane, 1 + 2 * core, 8, axis=0)
+    window = jnp.concatenate([lane[:, 0], lane[1:3, 1], lane[5:, 1]])
     line = jnp.stack([window] + others(window, 1))
     pieces = [line] + others(line, 4)
 
@@ -341,12 +344,13 @@
             jax.ShapeDtypeStruct((3, 3, 3, NY, NZ), jnp.float32),
             jax.ShapeDtypeStruct((16, 8, 128), jnp.float32),
         ),
-        in_specs=[smem, smem, vmem] + [vmem] * 4,
+        in_specs=[smem, smem, vmem, vmem] + [vmem] * 4,
         out_specs=(vmem, vmem),
         scratch_shapes=[pltpu.VMEM((LOADS, 13, 2, NZ), jnp.float32)]
         + [field(13), field(8), field(7), field(7), field(3, 7), field(3, 5), field(7, 12), field(5, 12)],
+        compiler_params=pltpu.CompilerParams(vmem_limit_bytes=12 << 20),
         name="krylov",
-    )(jnp.stack([slab, load]).astype(jnp.int32), patch_force[0], code, *pieces)
+    )(jnp.stack([slab, load]).astype(jnp.int32), patch_force[0], fixed_mask, patch_index, *pieces)
     parts = lax.all_to_all(moments, "space", 0, 0, tiled=True)
     displacement, energies = pl.pallas_call(
         combine_kernel,
@@ -357,6 +361,7 @@
         in_specs=[vmem, vmem],
         out_specs=(vmem, vmem),
         scratch_shapes=[field(3, 12), field(2)],
+        compiler_params=pltpu.CompilerParams(vmem_limit_bytes=6 << 20),
         name="combine",
     )(parts, basis)
     received = lax.all_to_all(energies, "load", 0, 0, tiled=True)

time: 74.8 us -> 68.9 us (0.921)
  waiting for transfers between devices: 13.4 us -> 10 us
  blocking collectives: 26.9 us -> 30 us
  local copies, waits for them, and re-layouts: 3.39 us -> 0.69 us
  Pallas kernels: 9.7 us -> 7.2 us
    ppermute x0 -> x3, starting transfers between devices: none -> 8.57 us  [the longest x1 3.99 us: shards(): below = lax.ppermute(chip, 'space', [(i, i + 2) for i in range(14)])]
    all_to_all x1 -> x0, starting transfers between devices: 7.33 us -> none  [shards(): lax.all_to_all(jnp.broadcast_to(own[None], (16,) + own.shape), 'space', 0...]
    all_to_all x1 -> x0, waiting for transfers between devices: 4.85 us -> none  [shards(): lax.all_to_all(jnp.broadcast_to(own[None], (16,) + own.shape), 'space', 0...]
    all_to_all x1, blocking collectives: 13.5 us -> 16.9 us  [shards(): parts = lax.all_to_all(moments, 'space', 0, 0, tiled=True)]
    unnamed x15 -> x9, local copies, waits for them, and re-layouts: 2.61 us -> 0.68 us
    pallas_call x1, Pallas kernels: 7.21 us -> 5.93 us  [shards(): pl.pallas_call(krylov_kernel, out_shape=(jax.ShapeDtypeStruct((3, 3, 3, N...]
    pallas_call x1, Pallas kernels: 2.48 us -> 1.27 us  [shards(): pl.pallas_call(combine_kernel, out_shape=(jax.ShapeDtypeStruct((3, 2, NY,...]
    ppermute x0 -> x3, waiting for transfers between devices: none -> 0.99 us  [the longest x1 0.83 us: shards(): partner = lax.ppermute(own, 'space', [(i, i ^ 1) for i in range(16)])]
  transfers between devices with their start and end apart: 7 -> 9, of which waited for: 5 -> 7; matrix products, arithmetic and copies ran while one was open for 2% -> 0% of each run, Pallas kernels for 0% -> 0%
where the time goes in v2:
time: 68.9 us; the launch traced here: 68.6 us
  blocking collectives  30 us (44%)
  starting transfers between devices  18.4 us (27%)
  waiting for transfers between devices  10 us (15%)
  Pallas kernels  7.2 us (10%)
  other arithmetic  1.62 us (2%)
  between operations  0.77 us (1%)
  local copies, waits for them, and re-layouts  0.69 us (1%)
    all_to_all x1, blocking collectives, shards(): parts = lax.all_to_all(moments, 'space', 0, 0, tiled=True)  16.9 us
    all_to_all x1, blocking collectives, shards(): received = lax.all_to_all(energies, 'load', 0, 0, tiled=True)  13.1 us
    ppermute x6, starting transfers between devices, others(): lax.ppermute(x, 'load', [(i, i ^ k * distance) for i in range(LOADS)])  9.82 us
    ppermute x6, waiting for transfers between devices, others(): lax.ppermute(x, 'load', [(i, i ^ k * distance) for i in range(LOADS)])  9.04 us
    pallas_call x1, Pallas kernels, shards(): pl.pallas_call(krylov_kernel, out_shape=(jax.ShapeDtypeStruct((3, 3, 3, N...  5.93 us
    ppermute x1, starting transfers between devices, shards(): below = lax.ppermute(chip, 'space', [(i, i + 2) for i in range(14)])  3.99 us
    ppermute x1, starting transfers between devices, shards(): partner = lax.ppermute(own, 'space', [(i, i ^ 1) for i in range(16)])  3.29 us
  transfers between devices with their start and end apart: 9, of which 7 were waited for; matrix products, arithmetic and copies ran while one was open for 0% of the time, Pallas kernels for 0%

profile of v2, /device:TPU:1, one launch (start us, length us, event | category | flops | bytes accessed | tf_op | source)
XLA Modules:
  0.0 68.6 jit_solution(14772343512020721823)
XLA Ops:
  0.6 0.0 copy-start.2
  0.6 0.8 %fusion.4 = f32[2,1,2,256]{3,2,0,1:T(2,128)S(1)} fusion(s32[2,32,256]{2,1,0:T(8,128)} %patches.1, s32[]{:T(128)S(6)} %select_n.32, s32[2,32,256]{2,1,0:T(8,128)} %fixed.1), kind=kLoop, calls=%fused_computation.17 | loop fusion | flops 4096 | bytes 12292 | tf_op jit(solution)/shard_map/stack | solution.py:327
  1.4 0.0 copy-done.2
  1.4 3.3 %collective-permute-start = (f32[2,2,2,256]{3,2,0,1:T(2,128)S(1)}, f32[2,2,2,256]{3,2,0,1:T(2,128)S(1)}, u32[]{:S(2)}, u32[]{:S(2)}) collective-permute-start(f32[2,2,2,256]{3,2,0,1:T(2,128)S(1)} %pad_maximum_fusion.3), channel_id=1, source_target_pairs={{0,1},{1,0},{2,3},{3,2},{4,5},{5,4},{6,7},{7,6},{8,9},{9,8},{10,11... | collective-permute-start | bytes 24584 | tf_op jit(solution)/shard_map/ppermute | solution.py:328
  4.7 0.8 %collective-permute-done = f32[2,2,2,256]{3,2,0,1:T(2,128)S(1)} collective-permute-done((f32[2,2,2,256]{3,2,0,1:T(2,128)S(1)}, f32[2,2,2,256]{3,2,0,1:T(2,128)S(1)}, u32[]{:S(2)}, u32[]{:S(2)}) %collective-permute-start) | collective-permute-done | bytes 8224 | tf_op jit(solution)/shard_map/ppermute | solution.py:328
  5.6 1.3 %collective-permute-start.2 = (f32[4,2,2,256]{3,2,0,1:T(2,128)S(1)}, f32[4,2,2,256]{3,2,0,1:T(2,128)S(1)}, u32[]{:S(2)}, u32[]{:S(2)}) collective-permute-start(f32[4,2,2,256]{3,2,0,1:T(2,128)S(1)} %pad_maximum_fusion.2), channel_id=1, source_target_pairs={{2,0},{3,1},{4,2},{5,3},{6,4},{7,5},{8,6},{9,7},{10,8},{11,9},{12,... | collective-permute-start | bytes 49160 | tf_op jit(solution)/shard_map/ppermute | solution.py:331
  6.9 4.0 %collective-permute-start.1 = (f32[4,2,2,256]{3,2,0,1:T(2,128)S(1)}, f32[4,2,2,256]{3,2,0,1:T(2,128)S(1)}, u32[]{:S(2)}, u32[]{:S(2)}) collective-permute-start(f32[4,2,2,256]{3,2,0,1:T(2,128)S(1)} %pad_maximum_fusion.2), channel_id=1, source_target_pairs={{0,2},{1,3},{2,4},{3,5},{4,6},{5,7},{6,8},{7,9},{8,10},{9,11},{10,... | collective-permute-start | bytes 49160 | tf_op jit(solution)/shard_map/ppermute | solution.py:330
  10.9 0.0 copy-start.3
  10.9 0.7 copy-done.3
  11.6 0.0 collective-permute-done.2
  11.6 0.2 collective-permute-done.1
  11.7 0.1 fusion.2
  11.8 5.3 %collective-permute-start.4 = (f32[13,2,256]{2,1,0:T(2,128)S(1)}, f32[13,2,256]{2,1,0:T(2,128)S(1)}, u32[]{:S(2)}, u32[]{:S(2)}) collective-permute-start(f32[13,2,256]{2,1,0:T(2,128)S(1)} %pad_maximum_fusion.1), channel_id=1, source_target_pairs={{0,32},{16,48},{32,0},{48,16},{64,96},{80,112},{96,64},{112,80},{1... | collective-permute-start | bytes 79880 | tf_op jit(solution)/shard_map/ppermute | solution.py:317
  17.1 1.2 %collective-permute-start.3 = (f32[13,2,256]{2,1,0:T(2,128)S(1)}, f32[13,2,256]{2,1,0:T(2,128)S(1)}, u32[]{:S(2)}, u32[]{:S(2)}) collective-permute-start(f32[13,2,256]{2,1,0:T(2,128)S(1)} %pad_maximum_fusion.1), channel_id=1, source_target_pairs={{0,16},{16,0},{32,48},{48,32},{64,80},{80,64},{96,112},{112,96},{1... | collective-permute-start | bytes 79880 | tf_op jit(solution)/shard_map/ppermute | solution.py:317
  18.3 0.0 collective-permute-start.5
  18.3 0.2 collective-permute-done.4
  18.5 2.2 %collective-permute-done.3 = f32[13,2,256]{2,1,0:T(2,128)S(1)} collective-permute-done((f32[13,2,256]{2,1,0:T(2,128)S(1)}, f32[13,2,256]{2,1,0:T(2,128)S(1)}, u32[]{:S(2)}, u32[]{:S(2)}) %collective-permute-start.3) | collective-permute-done | bytes 26656 | tf_op jit(solution)/shard_map/ppermute | solution.py:317
  20.8 2.4 %collective-permute-done.5 = f32[13,2,256]{2,1,0:T(2,128)S(1)} collective-permute-done((f32[13,2,256]{2,1,0:T(2,128)S(1)}, f32[13,2,256]{2,1,0:T(2,128)S(1)}, u32[]{:S(2)}, u32[]{:S(2)}) %collective-permute-start.5) | collective-permute-done | bytes 26656 | tf_op jit(solution)/shard_map/ppermute | solution.py:317
  23.1 0.0 copy-start
  23.1 0.0 copy-start.1
  23.1 0.1 pad_maximum_fusion.refs_0_
  23.2 2.6 %collective-permute-start.8 = (f32[4,13,2,256]{3,2,1,0:T(2,128)S(1)}, f32[4,13,2,256]{3,2,1,0:T(2,128)S(1)}, u32[]{:S(2)}, u32[]{:S(2)}) collective-permute-start(f32[4,13,2,256]{3,2,1,0:T(2,128)S(1)} %pad_maximum_fusion.refs_0_), channel_id=1, source_target_pairs={{0,192},{16,208},{32,224},{48,240},{64,128},{80,144},{96,160},{112... | collective-permute-start | bytes 319496 | tf_op jit(solution)/shard_map/ppermute | solution.py:317
  25.8 0.5 collective-permute-start.7
  26.3 0.3 collective-permute-start.6
  26.5 0.1 pad_add_fusion.place
  26.6 1.9 %collective-permute-done.8.refs_3_ = f32[4,13,2,256]{3,2,1,0:T(2,128)S(1)} collective-permute-done((f32[4,13,2,256]{3,2,1,0:T(2,128)S(1)}, f32[4,13,2,256]{3,2,1,0:T(2,128)S(1)}, u32[]{:S(2)}, u32[]{:S(2)}) %collective-permute-start.8) | collective-permute-done | bytes 106528 | tf_op jit(solution)/shard_map/ppermute | solution.py:317
  28.5 2.3 %collective-permute-done.7.refs_2_ = f32[4,13,2,256]{3,2,1,0:T(2,128)S(1)} collective-permute-done((f32[4,13,2,256]{3,2,1,0:T(2,128)S(1)}, f32[4,13,2,256]{3,2,1,0:T(2,128)S(1)}, u32[]{:S(2)}, u32[]{:S(2)}) %collective-permute-start.7) | collective-permute-done | bytes 106528 | tf_op jit(solution)/shard_map/ppermute | solution.py:317
  30.8 0.0 collective-permute-done.6.refs_1_
  30.8 0.0 copy-done
  30.8 0.0 copy-done.1
  30.9 5.9 %krylov.1 = (f32[3,3,3,32,256]{4,3,2,1,0:T(8,128)S(1)}, f32[16,8,128]{2,1,0:T(8,128)S(1)}) custom-call(s32[2]{0:T(128)S(1)} %pad_add_fusion.place, f32[3,16]{1,0:T(4,128)S(1)} %bitcast.20, s32[2,32,256]{2,1,0:T(8,128)S(1)} %copy-done, s32[2,32,256]{2,1,0:T(8,128)S(1)} %copy-done.1, f32[4,13,2,256]{3,2,1,0:T(2,128)S(1)} %pad_maximum_fusion.refs_0_, ...), custom_call_target="tpu_custom_call" | custom-call | tf_op jit(solution)/shard_map/krylov/pallas_call | solution.py:341
  36.8 16.9 %all_to_all.10.parts = f32[16,8,128]{2,1,0:T(8,128)S(1)} all-to-all(f32[16,8,128]{2,1,0:T(8,128)S(1)} %get-tuple-element.6), channel_id=1, replica_groups=mesh['load'=16,'space'=16] {'space'}, dimensions={0} | all-to-all | bytes 131072 | tf_op jit(solution)/shard_map/all_to_all | solution.py:354
  53.7 1.3 %combine.1 = (f32[3,2,32,256]{3,2,1,0:T(8,128)}, f32[16,2,2,256]{3,2,1,0:T(2,128)S(1)}) custom-call(f32[16,8,128]{2,1,0:T(8,128)S(1)} %all_to_all.10.parts, f32[3,3,3,32,256]{4,3,2,1,0:T(8,128)S(1)} %get-tuple-element.7.basis), custom_call_target="tpu_custom_call" | custom-call | tf_op jit(solution)/shard_map/combine/pallas_call | solution.py:355
  54.9 13.1 %all_to_all.11 = f32[16,2,2,256]{3,2,1,0:T(2,128)S(1)} all-to-all(f32[16,2,2,256]{3,2,1,0:T(2,128)S(1)} %get-tuple-element.9), channel_id=1, replica_groups=mesh['load'=16,'space'=16] {'load'}, dimensions={0} | all-to-all | bytes 131072 | tf_op jit(solution)/shard_map/all_to_all | solution.py:367
  68.0 0.6 multiply_multiply_fusion
  (10 shorter events, 0.1 us)
Async XLA Ops:
  0.6 0.8 %copy-start.2 = (f32[2,2,256]{2,1,0:T(2,128)S(1)}, f32[2,2,256]{2,1,0:T(2,128)}, u32[]{:S(2)}) copy-start(f32[2,2,256]{2,1,0:T(2,128)} %param.4) | copy-start | bytes 12292
  1.4 4.1 %collective-permute-start = (f32[2,2,2,256]{3,2,0,1:T(2,128)S(1)}, f32[2,2,2,256]{3,2,0,1:T(2,128)S(1)}, u32[]{:S(2)}, u32[]{:S(2)}) collective-permute-start(f32[2,2,2,256]{3,2,0,1:T(2,128)S(1)} %pad_maximum_fusion.3), channel_id=1, source_target_pairs={{0,1},{1,0},{2,3},{3,2},{4,5},{5,4},{6,7},{7,6},{8,9},{9,8},{10,11... | collective-permute-start | bytes 24584 | tf_op jit(solution)/shard_map/ppermute | solution.py:328
  5.6 6.0 %collective-permute-start.2 = (f32[4,2,2,256]{3,2,0,1:T(2,128)S(1)}, f32[4,2,2,256]{3,2,0,1:T(2,128)S(1)}, u32[]{:S(2)}, u32[]{:S(2)}) collective-permute-start(f32[4,2,2,256]{3,2,0,1:T(2,128)S(1)} %pad_maximum_fusion.2), channel_id=1, source_target_pairs={{2,0},{3,1},{4,2},{5,3},{6,4},{7,5},{8,6},{9,7},{10,8},{11,9},{12,... | collective-permute-start | bytes 49160 | tf_op jit(solution)/shard_map/ppermute | solution.py:331
  6.9 4.8 %collective-permute-start.1 = (f32[4,2,2,256]{3,2,0,1:T(2,128)S(1)}, f32[4,2,2,256]{3,2,0,1:T(2,128)S(1)}, u32[]{:S(2)}, u32[]{:S(2)}) collective-permute-start(f32[4,2,2,256]{3,2,0,1:T(2,128)S(1)} %pad_maximum_fusion.2), channel_id=1, source_target_pairs={{0,2},{1,3},{2,4},{3,5},{4,6},{5,7},{6,8},{7,9},{8,10},{9,11},{10,... | collective-permute-start | bytes 49160 | tf_op jit(solution)/shard_map/ppermute | solution.py:330
  10.9 0.7 copy-start.3
  11.8 6.7 %collective-permute-start.4 = (f32[13,2,256]{2,1,0:T(2,128)S(1)}, f32[13,2,256]{2,1,0:T(2,128)S(1)}, u32[]{:S(2)}, u32[]{:S(2)}) collective-permute-start(f32[13,2,256]{2,1,0:T(2,128)S(1)} %pad_maximum_fusion.1), channel_id=1, source_target_pairs={{0,32},{16,48},{32,0},{48,16},{64,96},{80,112},{96,64},{112,80},{1... | collective-permute-start | bytes 79880 | tf_op jit(solution)/shard_map/ppermute | solution.py:317
  17.1 3.6 %collective-permute-start.3 = (f32[13,2,256]{2,1,0:T(2,128)S(1)}, f32[13,2,256]{2,1,0:T(2,128)S(1)}, u32[]{:S(2)}, u32[]{:S(2)}) collective-permute-start(f32[13,2,256]{2,1,0:T(2,128)S(1)} %pad_maximum_fusion.1), channel_id=1, source_target_pairs={{0,16},{16,0},{32,48},{48,32},{64,80},{80,64},{96,112},{112,96},{1... | collective-permute-start | bytes 79880 | tf_op jit(solution)/shard_map/ppermute | solution.py:317
  18.3 4.8 %collective-permute-start.5 = (f32[13,2,256]{2,1,0:T(2,128)S(1)}, f32[13,2,256]{2,1,0:T(2,128)S(1)}, u32[]{:S(2)}, u32[]{:S(2)}) collective-permute-start(f32[13,2,256]{2,1,0:T(2,128)S(1)} %pad_maximum_fusion.1), channel_id=1, source_target_pairs={{0,48},{16,32},{32,16},{48,0},{64,112},{80,96},{96,80},{112,64},{1... | collective-permute-start | bytes 79880 | tf_op jit(solution)/shard_map/ppermute | solution.py:317
  23.1 7.7 %copy-start = (s32[2,32,256]{2,1,0:T(8,128)S(1)}, s32[2,32,256]{2,1,0:T(8,128)}, u32[]{:S(2)}) copy-start(s32[2,32,256]{2,1,0:T(8,128)} %fixed.1) | copy-start | bytes 196612
  23.1 7.7 %copy-start.1 = (s32[2,32,256]{2,1,0:T(8,128)S(1)}, s32[2,32,256]{2,1,0:T(8,128)}, u32[]{:S(2)}) copy-start(s32[2,32,256]{2,1,0:T(8,128)} %patches.1) | copy-start | bytes 196612
  23.2 5.4 %collective-permute-start.8 = (f32[4,13,2,256]{3,2,1,0:T(2,128)S(1)}, f32[4,13,2,256]{3,2,1,0:T(2,128)S(1)}, u32[]{:S(2)}, u32[]{:S(2)}) collective-permute-start(f32[4,13,2,256]{3,2,1,0:T(2,128)S(1)} %pad_maximum_fusion.refs_0_), channel_id=1, source_target_pairs={{0,192},{16,208},{32,224},{48,240},{64,128},{80,144},{96,160},{112... | collective-permute-start | bytes 319496 | tf_op jit(solution)/shard_map/ppermute | solution.py:317
  25.8 5.1 %collective-permute-start.7 = (f32[4,13,2,256]{3,2,1,0:T(2,128)S(1)}, f32[4,13,2,256]{3,2,1,0:T(2,128)S(1)}, u32[]{:S(2)}, u32[]{:S(2)}) collective-permute-start(f32[4,13,2,256]{3,2,1,0:T(2,128)S(1)} %pad_maximum_fusion.refs_0_), channel_id=1, source_target_pairs={{0,128},{16,144},{32,160},{48,176},{64,192},{80,208},{96,224},{112... | collective-permute-start | bytes 319496 | tf_op jit(solution)/shard_map/ppermute | solution.py:317
  26.3 4.6 %collective-permute-start.6 = (f32[4,13,2,256]{3,2,1,0:T(2,128)S(1)}, f32[4,13,2,256]{3,2,1,0:T(2,128)S(1)}, u32[]{:S(2)}, u32[]{:S(2)}) collective-permute-start(f32[4,13,2,256]{3,2,1,0:T(2,128)S(1)} %pad_maximum_fusion.refs_0_), channel_id=1, source_target_pairs={{0,64},{16,80},{32,96},{48,112},{64,0},{80,16},{96,32},{112,48},{1... | collective-permute-start | bytes 319496 | tf_op jit(solution)/shard_map/ppermute | solution.py:317

commit v3 on v2

--- a/solution.py
+++ b/solution.py
@@ -124,28 +124,42 @@
     return summed + (SHEAR / 3.0) * triple + DIAGONAL * corner
 
 
-def krylov_kernel(place, table, fixed, patches, *refs):
-    pieces, (basis, moments, staged, rows, weight, inverse, mass, w0, w1, planes, layers) = refs[:4], refs[4:]
-    own = place[1]
+def code_of(fixed, patch):
+    return jnp.where(fixed == 0, patch + 1, 0).astype(jnp.float32)
+
+
+def pack_kernel(gathered, density, fixed, patches, own, upper, lower, factor, rows):
+    for load in range(LOADS):
+        rows[:, 2 * load : 2 * load + 2, :] = gathered[load]
+    for i in range(2):
+        rho = rows[i]
+        layer = MODE_SCALE * (void_stiffness + (1.0 - void_stiffness) * (rho * rho * rho))
+        code = code_of(fixed[i], patches[i])
+        own[1 - i] = layer
+        own[2 + i] = code
+        if i == 0:
+            lower[0] = layer
+            lower[1] = code
+        else:
+            upper[0] = layer
+    mine = density[...]
+    factor[...] = (-3.0 * (1.0 - void_stiffness) / LOADS) * (mine * mine)
+
+
+def krylov_kernel(place, table, own, below, above, below_next, above_next, basis, moments, *scratch):
+    weight, codes, inverse, mass, w0, w1, planes, layers = scratch
     first = 2 * place[0] - 2
     y_first, y_last, z_first, z_last = plane_edges()
 
-    for far in range(4):
-        for near in range(4):
-            staged[own ^ (4 * far + near)] = pieces[far][near]
-    for load in range(LOADS):
-        rows[:, 2 * load : 2 * load + 2, :] = staged[load]
-
-    def set_weight(i, _):
-        layer = first - 1 + i
-        inside = jnp.where((layer >= 0) & (layer < NX), 1.0, 0.0)
-        rho = rows[i]
-        weight[i] = (MODE_SCALE * inside) * (void_stiffness + (1.0 - void_stiffness) * (rho * rho * rho))
-        return 0
-
-    lax.fori_loop(0, 8, set_weight, 0)
-
-    def set_plane(i, code):
+    layer_list = [(below_next, 0), (below, 1), (below, 0), (own, 1), (own, 0), (above, 1), (above, 0), (above_next, 0)]
+    code_list = [(below, 2), (below, 3), (own, 2), (own, 3), (above, 2), (above, 3), (above_next, 1)]
+    for target, offset, refs in ((weight, first - 1, layer_list), (codes, first, code_list)):
+        for i, (ref, k) in enumerate(refs):
+            inside = (offset + i >= 0) & (offset + i < NX)
+            target[i] = ref[k] if ref is own else ref[k] * jnp.where(inside, 1.0, 0.0)
+
+    def set_plane(i, _):
+        code = codes[i]
         both_layers = weight[i] + weight[i + 1]
         across = both_layers + prev_y(both_layers, y_first)
         diag = (DIAGONAL / MODE_SCALE) * (across + prev_z(across, z_first))
@@ -159,10 +173,9 @@
             force = [jnp.where(here, table[comp, patch], force[comp]) for comp in range(3)]
         for comp in range(3):
             w0[comp, i] = scaled * force[comp]
-
-    lax.fori_loop(0, 2, lambda i, _: (set_plane(i, rows[8 + i]), 0)[1], 0)
-    lax.fori_loop(2, 4, lambda i, _: (set_plane(i, jnp.where(fixed[i - 2] == 0, patches[i - 2] + 1, 0).astype(jnp.float32)), 0)[1], 0)
-    lax.fori_loop(4, 7, lambda i, _: (set_plane(i, rows[6 + i]), 0)[1], 0)
+        return 0
+
+    lax.fori_loop(0, 7, set_plane, 0)
 
     def to_modes(source, count):
         def body(i, _):
@@ -313,49 +326,39 @@
         energies[load] = energy[:, 2 * load : 2 * load + 2, :]
 
 
-def others(x, distance):
-    return [lax.ppermute(x, "load", [(i, i ^ (k * distance)) for i in range(LOADS)]) for k in range(1, 4)]
-
-
 def shards(density, fixed_mask, patch_index, patch_force):
     slab = lax.axis_index("space")
-    load = lax.axis_index("load")
-    core = slab % 2
-    fixed_rows = lax.dynamic_slice_in_dim(fixed_mask, 2 * load, 2, axis=1)
-    patch_rows = lax.dynamic_slice_in_dim(patch_index, 2 * load, 2, axis=1)
-    mine = jnp.where(fixed_rows == 0, patch_rows + 1, 0).astype(jnp.float32)
-    own = jnp.stack([density, mine], 1)
-    partner = lax.ppermute(own, "space", [(i, i ^ 1) for i in range(16)])
-    chip = jnp.concatenate([jnp.where(core == 0, own, partner), jnp.where(core == 0, partner, own)])
-    below = lax.ppermute(chip, "space", [(i, i + 2) for i in range(14)])
-    above = lax.ppermute(chip, "space", [(i + 2, i) for i in range(14)])
-    lane = jnp.concatenate([below, chip, above])
-    lane = lax.dynamic_slice_in_dim(lane, 1 + 2 * core, 8, axis=0)
-    window = jnp.concatenate([lane[:, 0], lane[1:3, 1], lane[5:, 1]])
-    line = jnp.stack([window] + others(window, 1))
-    pieces = [line] + others(line, 4)
-
     vmem = pl.BlockSpec(memory_space=pltpu.VMEM)
     smem = pl.BlockSpec(memory_space=pltpu.SMEM)
     field = lambda *shape: pltpu.VMEM(shape + (NY, NZ), jnp.float32)
+    planes = lambda *shape: jax.ShapeDtypeStruct(shape + (NY, NZ), jnp.float32)
+
+    gathered = lax.all_to_all(jnp.broadcast_to(density[None], (LOADS,) + density.shape), "load", 0, 0, tiled=True)
+    own, upper, lower, factor = pl.pallas_call(
+        pack_kernel,
+        out_shape=(planes(4), planes(1), planes(2), jax.ShapeDtypeStruct(density.shape, jnp.float32)),
+        in_specs=[vmem] * 4,
+        out_specs=(vmem,) * 4,
+        scratch_shapes=[field(2)],
+        compiler_params=pltpu.CompilerParams(vmem_limit_bytes=3 << 20),
+        name="pack",
+    )(gathered, density, fixed_mask, patch_index)
+    shifted = lambda x, by: lax.ppermute(x, "space", [(i, (i + by) % 16) for i in range(16)])
+    below, above, below_next, above_next = shifted(own, 1), shifted(own, -1), shifted(upper, 2), shifted(lower, -2)
     basis, moments = pl.pallas_call(
         krylov_kernel,
-        out_shape=(
-            jax.ShapeDtypeStruct((3, 3, 3, NY, NZ), jnp.float32),
-            jax.ShapeDtypeStruct((16, 8, 128), jnp.float32),
-        ),
-        in_specs=[smem, smem, vmem, vmem] + [vmem] * 4,
+        out_shape=(planes(3, 3, 3), jax.ShapeDtypeStruct((16, 8, 128), jnp.float32)),
+        in_specs=[smem, smem] + [vmem] * 5,
         out_specs=(vmem, vmem),
-        scratch_shapes=[pltpu.VMEM((LOADS, 13, 2, NZ), jnp.float32)]
-        + [field(13), field(8), field(7), field(7), field(3, 7), field(3, 5), field(7, 12), field(5, 12)],
+        scratch_shapes=[field(8), field(7), field(7), field(7), field(3, 7), field(3, 5), field(7, 12), field(5, 12)],
         compiler_params=pltpu.CompilerParams(vmem_limit_bytes=12 << 20),
         name="krylov",
-    )(jnp.stack([slab, load]).astype(jnp.int32), patch_force[0], fixed_mask, patch_index, *pieces)
+    )(slab.astype(jnp.int32).reshape(1), patch_force[0], own, below, above, below_next, above_next)
     parts = lax.all_to_all(moments, "space", 0, 0, tiled=True)
     displacement, energies = pl.pallas_call(
         combine_kernel,
         out_shape=(
-            jax.ShapeDtypeStruct((3, 2, NY, NZ), jnp.float32),
+            planes(3, 2),
             jax.ShapeDtypeStruct((LOADS, 2, 2, NZ), jnp.float32),
         ),
         in_specs=[vmem, vmem],
@@ -366,7 +369,7 @@
     )(parts, basis)
     received = lax.all_to_all(energies, "load", 0, 0, tiled=True)
     summed = jnp.sum(received, axis=0)
-    sensitivity = -3.0 * (1.0 - void_stiffness) * density**2 * (summed / LOADS)
+    sensitivity = factor * summed
     return (displacement[None], sensitivity)
 
 

time: 68.9 us -> 62.2 us (0.903)
  starting transfers between devices: 18.4 us -> 7.12 us
  blocking collectives: 30 us -> 40.8 us
  waiting for transfers between devices: 10 us -> 4.2 us
  other arithmetic: 1.62 us -> 0.63 us
  local copies, waits for them, and re-layouts: 0.69 us -> 1.47 us
    all_to_all x0 -> x1, blocking collectives: none -> 20.5 us  [shards(): lax.all_to_all(jnp.broadcast_to(density[None], (LOADS,) + density.shape),...]
    ppermute x9 -> x4, starting transfers between devices: 18.4 us -> 7.12 us  [shards(): lax.ppermute(x, 'space', [(i, (i + by) % 16) for i in range(16)])]
    all_to_all x1, blocking collectives: 16.9 us -> 8.51 us  [shards(): parts = lax.all_to_all(moments, 'space', 0, 0, tiled=True)]
    ppermute x9 -> x4, waiting for transfers between devices: 10 us -> 4.2 us  [shards(): lax.ppermute(x, 'space', [(i, (i + by) % 16) for i in range(16)])]
    all_to_all x1, blocking collectives: 13.1 us -> 11.8 us  [shards(): received = lax.all_to_all(energies, 'load', 0, 0, tiled=True)]
    another operation x5 -> x0, other arithmetic: 0.9 us -> none  [the longest x2 0.76 us: shards(): own = jnp.stack([density, mine], 1)]
    broadcast_in_dim x0 -> x1, local copies, waits for them, and re-layouts: none -> 0.77 us  [shards(): jnp.broadcast_to(density[None], (LOADS,) + density.shape)]
    pallas_call x2 -> x3, Pallas kernels: 7.2 us -> 6.99 us  [the longest x1 5.66 us: shards(): pl.pallas_call(krylov_kernel, out_shape=(planes(3, 3, 3), jax.ShapeDtypeS...]
  transfers between devices with their start and end apart: 9 -> 4, of which waited for: 7 -> 1; matrix products, arithmetic and copies ran while one was open for 0% -> 0% of each run, Pallas kernels for 0% -> 0%
where the time goes in v3:
time: 62.2 us; the launch traced here: 61.9 us
  blocking collectives  40.8 us (66%)
  starting transfers between devices  7.12 us (11%)
  Pallas kernels  6.99 us (11%)
  waiting for transfers between devices  4.2 us (7%)
  local copies, waits for them, and re-layouts  1.47 us (2%)
  between operations  0.68 us (1%)
  other arithmetic  0.63 us (1%)
    all_to_all x1, blocking collectives, shards(): lax.all_to_all(jnp.broadcast_to(density[None], (LOADS,) + density.shape),...  20.5 us
    all_to_all x1, blocking collectives, shards(): received = lax.all_to_all(energies, 'load', 0, 0, tiled=True)  11.8 us
    all_to_all x1, blocking collectives, shards(): parts = lax.all_to_all(moments, 'space', 0, 0, tiled=True)  8.51 us
    ppermute x4, starting transfers between devices, shards(): lax.ppermute(x, 'space', [(i, (i + by) % 16) for i in range(16)])  7.12 us
    pallas_call x1, Pallas kernels, shards(): pl.pallas_call(krylov_kernel, out_shape=(planes(3, 3, 3), jax.ShapeDtypeS...  5.66 us
    ppermute x4, waiting for transfers between devices, shards(): lax.ppermute(x, 'space', [(i, (i + by) % 16) for i in range(16)])  4.2 us
    pallas_call x1, Pallas kernels, shards(): pl.pallas_call(combine_kernel, out_shape=(planes(3, 2), jax.ShapeDtypeStr...  1.27 us
  transfers between devices with their start and end apart: 4, of which 1 were waited for; matrix products, arithmetic and copies ran while one was open for 0% of the time, Pallas kernels for 0%

profile of v3, /device:TPU:1, one launch (start us, length us, event | category | flops | bytes accessed | tf_op | source)
XLA Modules:
  0.0 61.9 jit_solution(2766832574947312372)
XLA Ops:
  0.6 0.0 copy-start.2
  0.6 0.8 %broadcast_in_dim.4 = f32[16,2,2,256]{3,2,1,0:T(2,128)S(1)} broadcast(f32[2,2,256]{2,1,0:T(2,128)} %density.1), dimensions={1,2,3} | broadcast | bytes 69632 | tf_op jit(solution)/shard_map/broadcast_in_dim | solution.py:336
  1.4 0.0 copy-start
  1.4 0.0 copy-start.1
  1.4 20.5 %all_to_all.15.gathered = f32[16,2,2,256]{3,2,1,0:T(2,128)S(1)} all-to-all(f32[16,2,2,256]{3,2,1,0:T(2,128)S(1)} %broadcast_in_dim.4), channel_id=1, replica_groups=mesh['load'=16,'space'=16] {'load'}, dimensions={0} | all-to-all | bytes 131072 | tf_op jit(solution)/shard_map/all_to_all | solution.py:336
  22.0 0.0 copy-done.2
  22.0 0.0 copy-done
  22.0 0.0 copy-done.1
  22.0 0.1 pack.1
  22.0 2.2 %collective-permute-start.1 = (f32[4,32,256]{2,1,0:T(8,128)S(1)}, f32[4,32,256]{2,1,0:T(8,128)S(1)}, u32[]{:S(2)}, u32[]{:S(2)}) collective-permute-start(f32[4,32,256]{2,1,0:T(8,128)S(1)} %get-tuple-element.10.own), channel_id=1, source_target_pairs={{0,15},{1,0},{2,1},{3,2},{4,3},{5,4},{6,5},{7,6},{8,7},{9,8},{10,9... | collective-permute-start | bytes 393224 | tf_op jit(solution)/shard_map/ppermute | solution.py:346
  24.2 0.8 %collective-permute-start = (f32[4,32,256]{2,1,0:T(8,128)S(1)}, f32[4,32,256]{2,1,0:T(8,128)S(1)}, u32[]{:S(2)}, u32[]{:S(2)}) collective-permute-start(f32[4,32,256]{2,1,0:T(8,128)S(1)} %get-tuple-element.10.own), channel_id=1, source_target_pairs={{0,1},{1,2},{2,3},{3,4},{4,5},{5,6},{6,7},{7,8},{8,9},{9,10},{10,1... | collective-permute-start | bytes 393224 | tf_op jit(solution)/shard_map/ppermute | solution.py:346
  25.0 4.2 %collective-permute-start.3 = (f32[2,32,256]{2,1,0:T(8,128)S(1)}, f32[2,32,256]{2,1,0:T(8,128)S(1)}, u32[]{:S(2)}, u32[]{:S(2)}) collective-permute-start(f32[2,32,256]{2,1,0:T(8,128)S(1)} %get-tuple-element.12), channel_id=1, source_target_pairs={{0,14},{1,15},{2,0},{3,1},{4,2},{5,3},{6,4},{7,5},{8,6},{9,7},{10,... | collective-permute-start | bytes 196616 | tf_op jit(solution)/shard_map/ppermute | solution.py:346
  29.1 0.0 collective-permute-start.2
  29.2 0.0 copy-start.3
  29.2 0.7 %copy-done.3 = f32[1,3,16]{2,0,1:T(1,128)S(1)} copy-done((f32[1,3,16]{2,0,1:T(1,128)S(1)}, f32[1,3,16]{2,0,1:T(1,128)}, u32[]{:S(2)}) %copy-start.3) | copy-done | bytes 216
  29.8 4.2 %collective-permute-done.2.below_next = f32[1,32,256]{2,1,0:T(8,128)S(1)} collective-permute-done((f32[1,32,256]{2,1,0:T(8,128)S(1)}, f32[1,32,256]{2,1,0:T(8,128)S(1)}, u32[]{:S(2)}, u32[]{:S(2)}) %collective-permute-start.2) | collective-permute-done | bytes 32800 | tf_op jit(solution)/shard_map/ppermute | solution.py:346
  34.0 0.0 collective-permute-done.3.above_next
  34.0 0.0 collective-permute-done.1.above
  34.0 0.0 collective-permute-done.below
  34.0 5.7 %krylov.1 = (f32[3,3,3,32,256]{4,3,2,1,0:T(8,128)S(1)}, f32[16,8,128]{2,1,0:T(8,128)S(1)}) custom-call(s32[1]{0:T(128)} %bitcast.place, f32[3,16]{1,0:T(4,128)S(1)} %bitcast.5, f32[4,32,256]{2,1,0:T(8,128)S(1)} %get-tuple-element.10.own, f32[4,32,256]{2,1,0:T(8,128)S(1)} %collective-permute-done.below, f32[4,32,256]{2,1,0:T(8,128)S(1)} %collective-permute-done.1.above, ...), custom_call_target="tpu_custom_call" | custom-call | tf_op jit(solution)/shard_map/krylov/pallas_call | solution.py:348
  39.7 8.5 %all_to_all.16.parts = f32[16,8,128]{2,1,0:T(8,128)S(1)} all-to-all(f32[16,8,128]{2,1,0:T(8,128)S(1)} %get-tuple-element.13), channel_id=1, replica_groups=mesh['load'=16,'space'=16] {'space'}, dimensions={0} | all-to-all | bytes 131072 | tf_op jit(solution)/shard_map/all_to_all | solution.py:357
  48.2 1.3 %combine.1 = (f32[3,2,32,256]{3,2,1,0:T(8,128)}, f32[16,2,2,256]{3,2,1,0:T(2,128)S(1)}) custom-call(f32[16,8,128]{2,1,0:T(8,128)S(1)} %all_to_all.16.parts, f32[3,3,3,32,256]{4,3,2,1,0:T(8,128)S(1)} %get-tuple-element.14.basis), custom_call_target="tpu_custom_call" | custom-call | tf_op jit(solution)/shard_map/combine/pallas_call | solution.py:358
  49.5 11.8 %all_to_all.17 = f32[16,2,2,256]{3,2,1,0:T(2,128)S(1)} all-to-all(f32[16,2,2,256]{3,2,1,0:T(2,128)S(1)} %get-tuple-element.17), channel_id=1, replica_groups=mesh['load'=16,'space'=16] {'load'}, dimensions={0} | all-to-all | bytes 131072 | tf_op jit(solution)/shard_map/all_to_all | solution.py:370
  61.3 0.6 mul.3
  (2 shorter events, 0.0 us)
Async XLA Ops:
  0.6 21.3 %copy-start.2 = (f32[2,2,256]{2,1,0:T(2,128)S(1)}, f32[2,2,256]{2,1,0:T(2,128)}, u32[]{:S(2)}) copy-start(f32[2,2,256]{2,1,0:T(2,128)} %density.1) | copy-start | bytes 12292
  1.4 20.6 %copy-start = (s32[2,32,256]{2,1,0:T(8,128)S(1)}, s32[2,32,256]{2,1,0:T(8,128)}, u32[]{:S(2)}) copy-start(s32[2,32,256]{2,1,0:T(8,128)} %fixed.1) | copy-start | bytes 196612
  1.4 20.5 %copy-start.1 = (s32[2,32,256]{2,1,0:T(8,128)S(1)}, s32[2,32,256]{2,1,0:T(8,128)}, u32[]{:S(2)}) copy-start(s32[2,32,256]{2,1,0:T(8,128)} %patches.1) | copy-start | bytes 196612
  22.0 12.0 %collective-permute-start.1 = (f32[4,32,256]{2,1,0:T(8,128)S(1)}, f32[4,32,256]{2,1,0:T(8,128)S(1)}, u32[]{:S(2)}, u32[]{:S(2)}) collective-permute-start(f32[4,32,256]{2,1,0:T(8,128)S(1)} %get-tuple-element.10.own), channel_id=1, source_target_pairs={{0,15},{1,0},{2,1},{3,2},{4,3},{5,4},{6,5},{7,6},{8,7},{9,8},{10,9... | collective-permute-start | bytes 393224 | tf_op jit(solution)/shard_map/ppermute | solution.py:346
  24.2 9.8 %collective-permute-start = (f32[4,32,256]{2,1,0:T(8,128)S(1)}, f32[4,32,256]{2,1,0:T(8,128)S(1)}, u32[]{:S(2)}, u32[]{:S(2)}) collective-permute-start(f32[4,32,256]{2,1,0:T(8,128)S(1)} %get-tuple-element.10.own), channel_id=1, source_target_pairs={{0,1},{1,2},{2,3},{3,4},{4,5},{5,6},{6,7},{7,8},{8,9},{9,10},{10,1... | collective-permute-start | bytes 393224 | tf_op jit(solution)/shard_map/ppermute | solution.py:346
  25.0 9.1 %collective-permute-start.3 = (f32[2,32,256]{2,1,0:T(8,128)S(1)}, f32[2,32,256]{2,1,0:T(8,128)S(1)}, u32[]{:S(2)}, u32[]{:S(2)}) collective-permute-start(f32[2,32,256]{2,1,0:T(8,128)S(1)} %get-tuple-element.12), channel_id=1, source_target_pairs={{0,14},{1,15},{2,0},{3,1},{4,2},{5,3},{6,4},{7,5},{8,6},{9,7},{10,... | collective-permute-start | bytes 196616 | tf_op jit(solution)/shard_map/ppermute | solution.py:346
  29.1 4.9 %collective-permute-start.2 = (f32[1,32,256]{2,1,0:T(8,128)S(1)}, f32[1,32,256]{2,1,0:T(8,128)S(1)}, u32[]{:S(2)}, u32[]{:S(2)}) collective-permute-start(f32[1,32,256]{2,1,0:T(8,128)S(1)} %get-tuple-element.11), channel_id=1, source_target_pairs={{0,2},{1,3},{2,4},{3,5},{4,6},{5,7},{6,8},{7,9},{8,10},{9,11},{10,... | collective-permute-start | bytes 98312 | tf_op jit(solution)/shard_map/ppermute | solution.py:346
  29.2 0.7 %copy-start.3 = (f32[1,3,16]{2,0,1:T(1,128)S(1)}, f32[1,3,16]{2,0,1:T(1,128)}, u32[]{:S(2)}) copy-start(f32[1,3,16]{2,0,1:T(1,128)} %param.7) | copy-start | bytes 580

commit v4 on v3

--- a/solution.py
+++ b/solution.py
@@ -167,15 +167,16 @@
         inverse[i] = inv
         mass[i] = diag
         scaled = inv * (1.0 + 2.0 * (first + i).astype(jnp.float32) / (NX - 1))
-        force = [jnp.zeros((NY, NZ), jnp.float32) for _ in range(3)]
-        for patch in range(PATCHES):
-            here = code == float(patch + 1)
-            force = [jnp.where(here, table[comp, patch], force[comp]) for comp in range(3)]
+        patch = code.astype(jnp.int32)
         for comp in range(3):
-            w0[comp, i] = scaled * force[comp]
+            row = jnp.broadcast_to(table[comp : comp + 1, :], (8, 128))
+            for y in range(0, NY, 8):
+                for z in range(0, NZ, 128):
+                    force = jnp.take_along_axis(row, patch[y : y + 8, z : z + 128], axis=1)
+                    w0[comp, i, y : y + 8, z : z + 128] = scaled[y : y + 8, z : z + 128] * force
         return 0
 
-    lax.fori_loop(0, 7, set_plane, 0)
+    lax.fori_loop(0, 7, set_plane, 0, unroll=True)
 
     def to_modes(source, count):
         def body(i, _):
@@ -184,7 +185,7 @@
                     planes[i, 4 * comp + k] = part
             return 0
 
-        lax.fori_loop(0, count, body, 0)
+        lax.fori_loop(0, count, body, 0, unroll=True)
 
     def shifted_operator(source, target, count, lead):
         to_modes(source, count + 2)
@@ -217,7 +218,7 @@
                     low = high
             return 0
 
-        lax.fori_loop(0, NY // 8, column, 0)
+        lax.fori_loop(0, NY // 8, column, 0, unroll=True)
 
         def to_nodes(i, _):
             inv = inverse[lead + i]
@@ -231,7 +232,7 @@
                 target[comp, i] = inv * force - source[comp, i + 1]
             return 0
 
-        lax.fori_loop(0, count, to_nodes, 0)
+        lax.fori_loop(0, count, to_nodes, 0, unroll=True)
 
     shifted_operator(w0, w1, 5, 1)
     shifted_operator(w1, basis.at[2], 3, 2)
@@ -252,7 +253,7 @@
         return summed
 
     totals = [jnp.zeros((8, 128), jnp.float32) for _ in range(5)]
-    totals.append(lax.fori_loop(0, NY // 8, column, jnp.zeros((8, 128), jnp.float32)))
+    totals.append(lax.fori_loop(0, NY // 8, column, jnp.zeros((8, 128), jnp.float32), unroll=True))
     for i in range(2):
         m = mass[2 + i]
         for comp in range(3):
@@ -321,7 +322,7 @@
                 low = high
         return 0
 
-    lax.fori_loop(0, NY // 8, column, 0)
+    lax.fori_loop(0, NY // 8, column, 0, unroll=True)
     for load in range(LOADS):
         energies[load] = energy[:, 2 * load : 2 * load + 2, :]
 
@@ -345,15 +346,16 @@
     )(gathered, density, fixed_mask, patch_index)
     shifted = lambda x, by: lax.ppermute(x, "space", [(i, (i + by) % 16) for i in range(16)])
     below, above, below_next, above_next = shifted(own, 1), shifted(own, -1), shifted(upper, 2), shifted(lower, -2)
+    table = jnp.pad(patch_force[0], ((0, 5), (1, 127 - PATCHES)))
     basis, moments = pl.pallas_call(
         krylov_kernel,
         out_shape=(planes(3, 3, 3), jax.ShapeDtypeStruct((16, 8, 128), jnp.float32)),
-        in_specs=[smem, smem] + [vmem] * 5,
+        in_specs=[smem] + [vmem] * 6,
         out_specs=(vmem, vmem),
         scratch_shapes=[field(8), field(7), field(7), field(7), field(3, 7), field(3, 5), field(7, 12), field(5, 12)],
         compiler_params=pltpu.CompilerParams(vmem_limit_bytes=12 << 20),
         name="krylov",
-    )(slab.astype(jnp.int32).reshape(1), patch_force[0], own, below, above, below_next, above_next)
+    )(slab.astype(jnp.int32).reshape(1), table, own, below, above, below_next, above_next)
     parts = lax.all_to_all(moments, "space", 0, 0, tiled=True)
     displacement, energies = pl.pallas_call(
         combine_kernel,

time: 62.2 us -> 59.7 us (0.960)
  Pallas kernels: 6.99 us -> 4.47 us
    pallas_call x1, Pallas kernels: 5.66 us -> 3.48 us  [shards(): pl.pallas_call(krylov_kernel, out_shape=(planes(3, 3, 3), jax.ShapeDtypeS...]
where the time goes in v4:
time: 59.7 us; the launch traced here: 59.4 us
  blocking collectives  40.8 us (68%)
  starting transfers between devices  7.12 us (12%)
  Pallas kernels  4.47 us (7%)
  waiting for transfers between devices  4.12 us (7%)
  local copies, waits for them, and re-layouts  1.54 us (3%)
  between operations  0.68 us (1%)
  other arithmetic  0.63 us (1%)
    all_to_all x1, blocking collectives, shards(): lax.all_to_all(jnp.broadcast_to(density[None], (LOADS,) + density.shape),...  20.5 us
    all_to_all x1, blocking collectives, shards(): received = lax.all_to_all(energies, 'load', 0, 0, tiled=True)  11.8 us
    all_to_all x1, blocking collectives, shards(): parts = lax.all_to_all(moments, 'space', 0, 0, tiled=True)  8.51 us
    ppermute x4, starting transfers between devices, shards(): lax.ppermute(x, 'space', [(i, (i + by) % 16) for i in range(16)])  7.12 us
    ppermute x4, waiting for transfers between devices, shards(): lax.ppermute(x, 'space', [(i, (i + by) % 16) for i in range(16)])  4.12 us
    pallas_call x1, Pallas kernels, shards(): pl.pallas_call(krylov_kernel, out_shape=(planes(3, 3, 3), jax.ShapeDtypeS...  3.48 us
  transfers between devices with their start and end apart: 4, of which 1 were waited for; matrix products, arithmetic and copies ran while one was open for 0% of the time, Pallas kernels for 0%

profile of v4, /device:TPU:1, one launch (start us, length us, event | category | flops | bytes accessed | tf_op | source)
XLA Modules:
  0.0 59.4 jit_solution(2815753156436192274)
XLA Ops:
  0.6 0.0 copy-start.2
  0.6 0.8 %broadcast_in_dim.4 = f32[16,2,2,256]{3,2,1,0:T(2,128)S(1)} broadcast(f32[2,2,256]{2,1,0:T(2,128)} %density.1), dimensions={1,2,3} | broadcast | bytes 69632 | tf_op jit(solution)/shard_map/broadcast_in_dim | solution.py:337
  1.4 0.0 copy-start
  1.4 0.0 copy-start.1
  1.4 20.5 %all_to_all.15.gathered = f32[16,2,2,256]{3,2,1,0:T(2,128)S(1)} all-to-all(f32[16,2,2,256]{3,2,1,0:T(2,128)S(1)} %broadcast_in_dim.4), channel_id=1, replica_groups=mesh['load'=16,'space'=16] {'load'}, dimensions={0} | all-to-all | bytes 131072 | tf_op jit(solution)/shard_map/all_to_all | solution.py:337
  22.0 0.0 copy-done.2
  22.0 0.0 copy-done
  22.0 0.0 copy-done.1
  22.0 0.1 pack.1
  22.0 2.2 %collective-permute-start.1 = (f32[4,32,256]{2,1,0:T(8,128)S(1)}, f32[4,32,256]{2,1,0:T(8,128)S(1)}, u32[]{:S(2)}, u32[]{:S(2)}) collective-permute-start(f32[4,32,256]{2,1,0:T(8,128)S(1)} %get-tuple-element.10.own), channel_id=1, source_target_pairs={{0,15},{1,0},{2,1},{3,2},{4,3},{5,4},{6,5},{7,6},{8,7},{9,8},{10,9... | collective-permute-start | bytes 393224 | tf_op jit(solution)/shard_map/ppermute | solution.py:347
  24.2 0.8 %collective-permute-start = (f32[4,32,256]{2,1,0:T(8,128)S(1)}, f32[4,32,256]{2,1,0:T(8,128)S(1)}, u32[]{:S(2)}, u32[]{:S(2)}) collective-permute-start(f32[4,32,256]{2,1,0:T(8,128)S(1)} %get-tuple-element.10.own), channel_id=1, source_target_pairs={{0,1},{1,2},{2,3},{3,4},{4,5},{5,6},{6,7},{7,8},{8,9},{9,10},{10,1... | collective-permute-start | bytes 393224 | tf_op jit(solution)/shard_map/ppermute | solution.py:347
  25.0 4.2 %collective-permute-start.3 = (f32[2,32,256]{2,1,0:T(8,128)S(1)}, f32[2,32,256]{2,1,0:T(8,128)S(1)}, u32[]{:S(2)}, u32[]{:S(2)}) collective-permute-start(f32[2,32,256]{2,1,0:T(8,128)S(1)} %get-tuple-element.12), channel_id=1, source_target_pairs={{0,14},{1,15},{2,0},{3,1},{4,2},{5,3},{6,4},{7,5},{8,6},{9,7},{10,... | collective-permute-start | bytes 196616 | tf_op jit(solution)/shard_map/ppermute | solution.py:347
  29.1 0.0 collective-permute-start.2
  29.2 0.0 copy-start.3
  29.2 0.7 %copy-done.3 = f32[1,3,16]{2,0,1:T(1,128)S(1)} copy-done((f32[1,3,16]{2,0,1:T(1,128)S(1)}, f32[1,3,16]{2,0,1:T(1,128)}, u32[]{:S(2)}) %copy-start.3) | copy-done | bytes 216
  29.8 0.1 pad.4.table
  29.9 4.1 %collective-permute-done.2.below_next = f32[1,32,256]{2,1,0:T(8,128)S(1)} collective-permute-done((f32[1,32,256]{2,1,0:T(8,128)S(1)}, f32[1,32,256]{2,1,0:T(8,128)S(1)}, u32[]{:S(2)}, u32[]{:S(2)}) %collective-permute-start.2) | collective-permute-done | bytes 32800 | tf_op jit(solution)/shard_map/ppermute | solution.py:347
  34.0 0.0 collective-permute-done.3.above_next
  34.0 0.0 collective-permute-done.1.above
  34.0 0.0 collective-permute-done.below
  34.0 3.5 %krylov.1 = (f32[3,3,3,32,256]{4,3,2,1,0:T(8,128)S(1)}, f32[16,8,128]{2,1,0:T(8,128)S(1)}) custom-call(s32[1]{0:T(128)} %bitcast.place, f32[8,128]{1,0:T(8,128)S(1)} %pad.4.table, f32[4,32,256]{2,1,0:T(8,128)S(1)} %get-tuple-element.10.own, f32[4,32,256]{2,1,0:T(8,128)S(1)} %collective-permute-done.below, f32[4,32,256]{2,1,0:T(8,128)S(1)} %collective-permute-done.1.above, ...), custom_call_target="tpu_custom_call" | custom-call | tf_op jit(solution)/shard_map/krylov/pallas_call | solution.py:350
  37.5 8.5 %all_to_all.16.parts = f32[16,8,128]{2,1,0:T(8,128)S(1)} all-to-all(f32[16,8,128]{2,1,0:T(8,128)S(1)} %get-tuple-element.13), channel_id=1, replica_groups=mesh['load'=16,'space'=16] {'space'}, dimensions={0} | all-to-all | bytes 131072 | tf_op jit(solution)/shard_map/all_to_all | solution.py:359
  46.0 0.9 %combine.1 = (f32[3,2,32,256]{3,2,1,0:T(8,128)}, f32[16,2,2,256]{3,2,1,0:T(2,128)S(1)}) custom-call(f32[16,8,128]{2,1,0:T(8,128)S(1)} %all_to_all.16.parts, f32[3,3,3,32,256]{4,3,2,1,0:T(8,128)S(1)} %get-tuple-element.14.basis), custom_call_target="tpu_custom_call" | custom-call | tf_op jit(solution)/shard_map/combine/pallas_call | solution.py:360
  47.0 11.8 %all_to_all.17 = f32[16,2,2,256]{3,2,1,0:T(2,128)S(1)} all-to-all(f32[16,2,2,256]{3,2,1,0:T(2,128)S(1)} %get-tuple-element.17), channel_id=1, replica_groups=mesh['load'=16,'space'=16] {'load'}, dimensions={0} | all-to-all | bytes 131072 | tf_op jit(solution)/shard_map/all_to_all | solution.py:372
  58.8 0.6 %mul.3 = f32[2,2,256]{2,1,0:T(2,128)} multiply(f32[2,2,256]{2,1,0:T(2,128)S(1)} %get-tuple-element.16, f32[2,2,256]{2,1,0:T(2,128)S(1)} %reduce_sum.9) | non-fusion elementwise | flops 1024 | bytes 12288 | tf_op jit(solution)/shard_map/mul | solution.py:374
  (2 shorter events, 0.0 us)
Async XLA Ops:
  0.6 21.3 %copy-start.2 = (f32[2,2,256]{2,1,0:T(2,128)S(1)}, f32[2,2,256]{2,1,0:T(2,128)}, u32[]{:S(2)}) copy-start(f32[2,2,256]{2,1,0:T(2,128)} %density.1) | copy-start | bytes 12292
  1.4 20.6 %copy-start = (s32[2,32,256]{2,1,0:T(8,128)S(1)}, s32[2,32,256]{2,1,0:T(8,128)}, u32[]{:S(2)}) copy-start(s32[2,32,256]{2,1,0:T(8,128)} %fixed.1) | copy-start | bytes 196612
  1.4 20.5 %copy-start.1 = (s32[2,32,256]{2,1,0:T(8,128)S(1)}, s32[2,32,256]{2,1,0:T(8,128)}, u32[]{:S(2)}) copy-start(s32[2,32,256]{2,1,0:T(8,128)} %patches.1) | copy-start | bytes 196612
  22.0 12.0 %collective-permute-start.1 = (f32[4,32,256]{2,1,0:T(8,128)S(1)}, f32[4,32,256]{2,1,0:T(8,128)S(1)}, u32[]{:S(2)}, u32[]{:S(2)}) collective-permute-start(f32[4,32,256]{2,1,0:T(8,128)S(1)} %get-tuple-element.10.own), channel_id=1, source_target_pairs={{0,15},{1,0},{2,1},{3,2},{4,3},{5,4},{6,5},{7,6},{8,7},{9,8},{10,9... | collective-permute-start | bytes 393224 | tf_op jit(solution)/shard_map/ppermute | solution.py:347
  24.2 9.8 %collective-permute-start = (f32[4,32,256]{2,1,0:T(8,128)S(1)}, f32[4,32,256]{2,1,0:T(8,128)S(1)}, u32[]{:S(2)}, u32[]{:S(2)}) collective-permute-start(f32[4,32,256]{2,1,0:T(8,128)S(1)} %get-tuple-element.10.own), channel_id=1, source_target_pairs={{0,1},{1,2},{2,3},{3,4},{4,5},{5,6},{6,7},{7,8},{8,9},{9,10},{10,1... | collective-permute-start | bytes 393224 | tf_op jit(solution)/shard_map/ppermute | solution.py:347
  25.0 9.1 %collective-permute-start.3 = (f32[2,32,256]{2,1,0:T(8,128)S(1)}, f32[2,32,256]{2,1,0:T(8,128)S(1)}, u32[]{:S(2)}, u32[]{:S(2)}) collective-permute-start(f32[2,32,256]{2,1,0:T(8,128)S(1)} %get-tuple-element.12), channel_id=1, source_target_pairs={{0,14},{1,15},{2,0},{3,1},{4,2},{5,3},{6,4},{7,5},{8,6},{9,7},{10,... | collective-permute-start | bytes 196616 | tf_op jit(solution)/shard_map/ppermute | solution.py:347
  29.1 4.9 %collective-permute-start.2 = (f32[1,32,256]{2,1,0:T(8,128)S(1)}, f32[1,32,256]{2,1,0:T(8,128)S(1)}, u32[]{:S(2)}, u32[]{:S(2)}) collective-permute-start(f32[1,32,256]{2,1,0:T(8,128)S(1)} %get-tuple-element.11), channel_id=1, source_target_pairs={{0,2},{1,3},{2,4},{3,5},{4,6},{5,7},{6,8},{7,9},{8,10},{9,11},{10,... | collective-permute-start | bytes 98312 | tf_op jit(solution)/shard_map/ppermute | solution.py:347
  29.2 0.7 %copy-start.3 = (f32[1,3,16]{2,0,1:T(1,128)S(1)}, f32[1,3,16]{2,0,1:T(1,128)}, u32[]{:S(2)}) copy-start(f32[1,3,16]{2,0,1:T(1,128)} %param.7) | copy-start | bytes 580

commit v5 on v4

--- a/solution.py
+++ b/solution.py
@@ -281,17 +281,20 @@
                 summed = term if summed is None else summed + term
         return summed
 
+    def ratio(top, bottom):
+        return jnp.where((top > 0.0) & (bottom > 0.0), top / bottom, 0.0)
+
     first = nu[0] / eta[0]
     z = [1.0 - first, -first]
     now = form(z, nu)
     beta = now / nu[0]
     p = [z[0] + beta, z[1]]
-    second = now / form(p, eta)
+    second = ratio(now, form(p, eta))
     last = [z[0] - second * p[0], z[1] - second * (p[0] + p[1]), -(second * p[1])]
-    then = form(last, nu)
-    beta = then / now
+    then = jnp.where(second > 0.0, form(last, nu), 0.0)
+    beta = ratio(then, now)
     q = [last[0] + beta * p[0], last[1] + beta * p[1], last[2]]
-    third = then / form(q, eta)
+    third = ratio(then, form(q, eta))
     return [first + second * p[0] + third * q[0], second * p[1] + third * q[1], third * q[2]]
 
 

time: 59.7 us -> 59.7 us (level)
  no operation moved by 1% of the time
where the time goes in v5:
time: 59.7 us; the launch traced here: 59.4 us
  blocking collectives  40.8 us (68%)
  starting transfers between devices  7.12 us (12%)
  Pallas kernels  4.48 us (8%)
  waiting for transfers between devices  4.12 us (7%)
  local copies, waits for them, and re-layouts  1.54 us (3%)
  between operations  0.68 us (1%)
  other arithmetic  0.63 us (1%)
    all_to_all x1, blocking collectives, shards(): lax.all_to_all(jnp.broadcast_to(density[None], (LOADS,) + density.shape),...  20.5 us
    all_to_all x1, blocking collectives, shards(): received = lax.all_to_all(energies, 'load', 0, 0, tiled=True)  11.8 us
    all_to_all x1, blocking collectives, shards(): parts = lax.all_to_all(moments, 'space', 0, 0, tiled=True)  8.51 us
    ppermute x4, starting transfers between devices, shards(): lax.ppermute(x, 'space', [(i, (i + by) % 16) for i in range(16)])  7.12 us
    ppermute x4, waiting for transfers between devices, shards(): lax.ppermute(x, 'space', [(i, (i + by) % 16) for i in range(16)])  4.12 us
    pallas_call x1, Pallas kernels, shards(): pl.pallas_call(krylov_kernel, out_shape=(planes(3, 3, 3), jax.ShapeDtypeS...  3.48 us
  transfers between devices with their start and end apart: 4, of which 1 were waited for; matrix products, arithmetic and copies ran while one was open for 0% of the time, Pallas kernels for 0%

profile of v5, /device:TPU:1, one launch (start us, length us, event | category | flops | bytes accessed | tf_op | source)
XLA Modules:
  0.0 59.4 jit_solution(12203512201904793010)
XLA Ops:
  0.6 0.0 copy-start.2
  0.6 0.8 %broadcast_in_dim.4 = f32[16,2,2,256]{3,2,1,0:T(2,128)S(1)} broadcast(f32[2,2,256]{2,1,0:T(2,128)} %density.1), dimensions={1,2,3} | broadcast | bytes 69632 | tf_op jit(solution)/shard_map/broadcast_in_dim | solution.py:340
  1.4 0.0 copy-start
  1.4 0.0 copy-start.1
  1.4 20.5 %all_to_all.15.gathered = f32[16,2,2,256]{3,2,1,0:T(2,128)S(1)} all-to-all(f32[16,2,2,256]{3,2,1,0:T(2,128)S(1)} %broadcast_in_dim.4), channel_id=1, replica_groups=mesh['load'=16,'space'=16] {'load'}, dimensions={0} | all-to-all | bytes 131072 | tf_op jit(solution)/shard_map/all_to_all | solution.py:340
  22.0 0.0 copy-done.2
  22.0 0.0 copy-done
  22.0 0.0 copy-done.1
  22.0 0.1 pack.1
  22.0 2.2 %collective-permute-start.1 = (f32[4,32,256]{2,1,0:T(8,128)S(1)}, f32[4,32,256]{2,1,0:T(8,128)S(1)}, u32[]{:S(2)}, u32[]{:S(2)}) collective-permute-start(f32[4,32,256]{2,1,0:T(8,128)S(1)} %get-tuple-element.10.own), channel_id=1, source_target_pairs={{0,15},{1,0},{2,1},{3,2},{4,3},{5,4},{6,5},{7,6},{8,7},{9,8},{10,9... | collective-permute-start | bytes 393224 | tf_op jit(solution)/shard_map/ppermute | solution.py:350
  24.2 0.8 %collective-permute-start = (f32[4,32,256]{2,1,0:T(8,128)S(1)}, f32[4,32,256]{2,1,0:T(8,128)S(1)}, u32[]{:S(2)}, u32[]{:S(2)}) collective-permute-start(f32[4,32,256]{2,1,0:T(8,128)S(1)} %get-tuple-element.10.own), channel_id=1, source_target_pairs={{0,1},{1,2},{2,3},{3,4},{4,5},{5,6},{6,7},{7,8},{8,9},{9,10},{10,1... | collective-permute-start | bytes 393224 | tf_op jit(solution)/shard_map/ppermute | solution.py:350
  25.0 4.2 %collective-permute-start.3 = (f32[2,32,256]{2,1,0:T(8,128)S(1)}, f32[2,32,256]{2,1,0:T(8,128)S(1)}, u32[]{:S(2)}, u32[]{:S(2)}) collective-permute-start(f32[2,32,256]{2,1,0:T(8,128)S(1)} %get-tuple-element.12), channel_id=1, source_target_pairs={{0,14},{1,15},{2,0},{3,1},{4,2},{5,3},{6,4},{7,5},{8,6},{9,7},{10,... | collective-permute-start | bytes 196616 | tf_op jit(solution)/shard_map/ppermute | solution.py:350
  29.1 0.0 collective-permute-start.2
  29.2 0.0 copy-start.3
  29.2 0.7 %copy-done.3 = f32[1,3,16]{2,0,1:T(1,128)S(1)} copy-done((f32[1,3,16]{2,0,1:T(1,128)S(1)}, f32[1,3,16]{2,0,1:T(1,128)}, u32[]{:S(2)}) %copy-start.3) | copy-done | bytes 216
  29.8 0.1 pad.4.table
  29.9 4.1 %collective-permute-done.2.below_next = f32[1,32,256]{2,1,0:T(8,128)S(1)} collective-permute-done((f32[1,32,256]{2,1,0:T(8,128)S(1)}, f32[1,32,256]{2,1,0:T(8,128)S(1)}, u32[]{:S(2)}, u32[]{:S(2)}) %collective-permute-start.2) | collective-permute-done | bytes 32800 | tf_op jit(solution)/shard_map/ppermute | solution.py:350
  34.0 0.0 collective-permute-done.3.above_next
  34.0 0.0 collective-permute-done.1.above
  34.0 0.0 collective-permute-done.below
  34.0 3.5 %krylov.1 = (f32[3,3,3,32,256]{4,3,2,1,0:T(8,128)S(1)}, f32[16,8,128]{2,1,0:T(8,128)S(1)}) custom-call(s32[1]{0:T(128)} %bitcast.place, f32[8,128]{1,0:T(8,128)S(1)} %pad.4.table, f32[4,32,256]{2,1,0:T(8,128)S(1)} %get-tuple-element.10.own, f32[4,32,256]{2,1,0:T(8,128)S(1)} %collective-permute-done.below, f32[4,32,256]{2,1,0:T(8,128)S(1)} %collective-permute-done.1.above, ...), custom_call_target="tpu_custom_call" | custom-call | tf_op jit(solution)/shard_map/krylov/pallas_call | solution.py:353
  37.5 8.5 %all_to_all.16.parts = f32[16,8,128]{2,1,0:T(8,128)S(1)} all-to-all(f32[16,8,128]{2,1,0:T(8,128)S(1)} %get-tuple-element.13), channel_id=1, replica_groups=mesh['load'=16,'space'=16] {'space'}, dimensions={0} | all-to-all | bytes 131072 | tf_op jit(solution)/shard_map/all_to_all | solution.py:362
  46.0 0.9 %combine.1 = (f32[3,2,32,256]{3,2,1,0:T(8,128)}, f32[16,2,2,256]{3,2,1,0:T(2,128)S(1)}) custom-call(f32[16,8,128]{2,1,0:T(8,128)S(1)} %all_to_all.16.parts, f32[3,3,3,32,256]{4,3,2,1,0:T(8,128)S(1)} %get-tuple-element.14.basis), custom_call_target="tpu_custom_call" | custom-call | tf_op jit(solution)/shard_map/combine/pallas_call | solution.py:363
  47.0 11.8 %all_to_all.17 = f32[16,2,2,256]{3,2,1,0:T(2,128)S(1)} all-to-all(f32[16,2,2,256]{3,2,1,0:T(2,128)S(1)} %get-tuple-element.17), channel_id=1, replica_groups=mesh['load'=16,'space'=16] {'load'}, dimensions={0} | all-to-all | bytes 131072 | tf_op jit(solution)/shard_map/all_to_all | solution.py:375
  58.8 0.6 %mul.3 = f32[2,2,256]{2,1,0:T(2,128)} multiply(f32[2,2,256]{2,1,0:T(2,128)S(1)} %get-tuple-element.16, f32[2,2,256]{2,1,0:T(2,128)S(1)} %reduce_sum.9) | non-fusion elementwise | flops 1024 | bytes 12288 | tf_op jit(solution)/shard_map/mul | solution.py:377
  (2 shorter events, 0.0 us)
Async XLA Ops:
  0.6 21.3 %copy-start.2 = (f32[2,2,256]{2,1,0:T(2,128)S(1)}, f32[2,2,256]{2,1,0:T(2,128)}, u32[]{:S(2)}) copy-start(f32[2,2,256]{2,1,0:T(2,128)} %density.1) | copy-start | bytes 12292
  1.4 20.6 %copy-start = (s32[2,32,256]{2,1,0:T(8,128)S(1)}, s32[2,32,256]{2,1,0:T(8,128)}, u32[]{:S(2)}) copy-start(s32[2,32,256]{2,1,0:T(8,128)} %fixed.1) | copy-start | bytes 196612
  1.4 20.5 %copy-start.1 = (s32[2,32,256]{2,1,0:T(8,128)S(1)}, s32[2,32,256]{2,1,0:T(8,128)}, u32[]{:S(2)}) copy-start(s32[2,32,256]{2,1,0:T(8,128)} %patches.1) | copy-start | bytes 196612
  22.0 12.0 %collective-permute-start.1 = (f32[4,32,256]{2,1,0:T(8,128)S(1)}, f32[4,32,256]{2,1,0:T(8,128)S(1)}, u32[]{:S(2)}, u32[]{:S(2)}) collective-permute-start(f32[4,32,256]{2,1,0:T(8,128)S(1)} %get-tuple-element.10.own), channel_id=1, source_target_pairs={{0,15},{1,0},{2,1},{3,2},{4,3},{5,4},{6,5},{7,6},{8,7},{9,8},{10,9... | collective-permute-start | bytes 393224 | tf_op jit(solution)/shard_map/ppermute | solution.py:350
  24.2 9.8 %collective-permute-start = (f32[4,32,256]{2,1,0:T(8,128)S(1)}, f32[4,32,256]{2,1,0:T(8,128)S(1)}, u32[]{:S(2)}, u32[]{:S(2)}) collective-permute-start(f32[4,32,256]{2,1,0:T(8,128)S(1)} %get-tuple-element.10.own), channel_id=1, source_target_pairs={{0,1},{1,2},{2,3},{3,4},{4,5},{5,6},{6,7},{7,8},{8,9},{9,10},{10,1... | collective-permute-start | bytes 393224 | tf_op jit(solution)/shard_map/ppermute | solution.py:350
  25.0 9.1 %collective-permute-start.3 = (f32[2,32,256]{2,1,0:T(8,128)S(1)}, f32[2,32,256]{2,1,0:T(8,128)S(1)}, u32[]{:S(2)}, u32[]{:S(2)}) collective-permute-start(f32[2,32,256]{2,1,0:T(8,128)S(1)} %get-tuple-element.12), channel_id=1, source_target_pairs={{0,14},{1,15},{2,0},{3,1},{4,2},{5,3},{6,4},{7,5},{8,6},{9,7},{10,... | collective-permute-start | bytes 196616 | tf_op jit(solution)/shard_map/ppermute | solution.py:350
  29.1 4.9 %collective-permute-start.2 = (f32[1,32,256]{2,1,0:T(8,128)S(1)}, f32[1,32,256]{2,1,0:T(8,128)S(1)}, u32[]{:S(2)}, u32[]{:S(2)}) collective-permute-start(f32[1,32,256]{2,1,0:T(8,128)S(1)} %get-tuple-element.11), channel_id=1, source_target_pairs={{0,2},{1,3},{2,4},{3,5},{4,6},{5,7},{6,8},{7,9},{8,10},{9,11},{10,... | collective-permute-start | bytes 98312 | tf_op jit(solution)/shard_map/ppermute | solution.py:350
  29.2 0.7 %copy-start.3 = (f32[1,3,16]{2,0,1:T(1,128)S(1)}, f32[1,3,16]{2,0,1:T(1,128)}, u32[]{:S(2)}) copy-start(f32[1,3,16]{2,0,1:T(1,128)} %param.7) | copy-start | bytes 580
